TPU v7x, 128 devices: a whole 4x4x4 slice. The times are simulated.
128 devices in a mesh: gx: 32 (over x, z_lo, y), gy: 4 (over z_hi, core).
Axes of the slice: x: 4, y: 4, z: 4 (z_hi: 2, z_lo: 2; z = z_hi * 2 + z_lo), core: 2. Of those that a mesh axis runs over, the one named last changes fastest.
Arguments:
- particles: bfloat16 [65536, 128], P(('gx', 'gy')), may hold values from -6 to 6
- send_counts: int32 [128, 128], P(('gx', 'gy')), may hold values from 0 to 8, as said below
- cell_lists: int32 [128, 1024], P(('gx', 'gy')), may hold values from 0 to 4095
- base_field: bfloat16 [64, 32, 64, 256], P(None, 'gx', 'gy'), may hold values from -6 to 6
- proj_weight: bfloat16 [128, 64], replicated, may hold values from -0.5 to 0.5
- conv_weight: bfloat16 [27, 64, 64], replicated, may hold values from -0.15625 to 0.15625
- cotangent: bfloat16 [64, 32, 64, 256], P(None, 'gx', 'gy'), may hold values from -6 to 6
Outputs:
- out_field: bfloat16 [64, 32, 64, 256], P(None, 'gx', 'gy')
- row_grads: float32 [65536, 128], P(('gx', 'gy'))
- conv_grad: float32 [27, 64, 64], replicated
- proj_grad: float32 [128, 64], replicated
Inputs may be any that keep to these rules, and one draw needn't show every extreme that they name: `send_counts`: row s holds how many of source s's 512 rows go to each owner; each row sums to 512; source s's particle rows are listed grouped by owner in increasing order; at most 8 from one source to one owner, and some owner receives 8 from every source. `cell_lists`: entry s * 8 + r of owner d's row is the local cell of the r-th row that source s sends to d; entries of unused slots are ignored.
All inputs are finite; a program needn't handle non-finite values.
Results may differ from a plain program's by a relative error of at most 0.0041.
Values may be sent and summed in bfloat16 or wider, within the bound.
A program may use at most 64 MiB of HBM per device.

v0:
```python
import functools
import math

import jax
import jax.numpy as jnp
from jax import lax
from jax.experimental import pallas as pl
from jax.experimental.pallas import tpu as pltpu
from jax.sharding import PartitionSpec as P

MESH = pl.DeviceIdType.MESH
F32 = jnp.float32
BF16 = jnp.bfloat16

F_CHUNKS = ((0, 4), (12, 4), (4, 4), (8, 4))
F_ROWS = ((0, 3), (13, 3), (3, 4), (7, 6))
G_ROWS = ((0, 2), (14, 2), (2, 4), (6, 8))
N_TAPS = 9


def nt_dot(a, b):
    return lax.dot_general(a, b, (((1,), (1,)), ((), ())), preferred_element_type=F32)


def roll_z(x, shift):
    return pltpu.roll(x, shift % x.shape[1], 1)


def kernel(
    ngx,
    ngy,
    counts_ref,
    cells_ref,
    rows_ref,
    base_ref,
    cot_ref,
    wf_ref,
    wb_ref,
    wp_ref,
    wpt_ref,
    out_ref,
    rowg_ref,
    convg_ref,
    projg_ref,
    send,
    arr,
    onehot_t,
    paint_a,
    paint_b,
    fld,
    pgr,
    fg,
    sgt,
    acc,
    tiles,
    rs,
    ag,
    sgs,
    sgr,
    a2a_sem,
    rev_sem,
    rs_sem,
    ag_sem,
    fx_send,
    fx_recv,
    fy_send,
    fy_recv,
    gx_send,
    gx_recv,
    gy_send,
    gy_recv,
):
    n = ngx * ngy
    nrows, feats = rows_ref.shape
    cy, chans, nz = base_ref.shape
    nslots = cells_ref.shape[1]
    cap = nslots // n
    ntile = tiles.shape[0] * tiles.shape[1]
    per = tiles.shape[1]
    nconv = 120 // per
    gi = lax.axis_index("gx")
    gj = lax.axis_index("gy")
    me = gi * ngy + gj

    def coords(d):
        return (lax.div(d, ngy), lax.rem(d, ngy))

    def peer_of(k):
        return lax.rem(me + k, n)

    barrier = pltpu.get_barrier_semaphore()

    @pl.loop(1, n)
    def _(k):
        pl.semaphore_signal(barrier, inc=1, device_id=coords(peer_of(k)), device_id_type=MESH)

    counts = counts_ref[...].astype(F32)
    lane = lax.broadcasted_iota(jnp.int32, (nslots, n), 1)
    slot = lax.broadcasted_iota(jnp.int32, (nslots, n), 0)
    owner = lax.div(slot, cap)
    offs = jnp.sum(jnp.where(lane < owner, counts, 0.0), axis=1, keepdims=True)
    mine = jnp.sum(jnp.where(lane == owner, counts, 0.0), axis=1, keepdims=True)
    place = (slot - owner * cap)[:, :1]
    index = jnp.where(place < mine.astype(jnp.int32), offs.astype(jnp.int32) + place, -1)
    pick = lax.broadcasted_iota(jnp.int32, (nslots, nrows), 1) == index
    outgoing = jnp.dot(pick.astype(F32).astype(BF16), rows_ref[...], preferred_element_type=F32)
    send[...] = outgoing.astype(BF16).reshape(send.shape)

    pl.semaphore_wait(barrier, n - 1)

    def spread(src, dst, sems):
        @pl.loop(1, n)
        def _(k):
            peer = peer_of(k)
            pltpu.make_async_remote_copy(
                src_ref=src.at[peer],
                dst_ref=dst.at[me],
                send_sem=sems.at[0],
                recv_sem=sems.at[1],
                device_id=coords(peer),
                device_id_type=MESH,
            ).start()

        dst[pl.ds(me, 1)] = src[pl.ds(me, 1)]

    def waits(src, dst, sems, count):
        return pltpu.make_async_remote_copy(
            src_ref=src.at[pl.ds(0, count)],
            dst_ref=dst.at[pl.ds(0, count)],
            send_sem=sems.at[0],
            recv_sem=sems.at[1],
            device_id=coords(peer_of(1)),
            device_id_type=MESH,
        )

    spread(send, arr, a2a_sem)

    counts_b = jnp.broadcast_to(counts, (8, n)).astype(BF16)
    upper = lax.broadcasted_iota(jnp.int32, (n, n), 0) <= lax.broadcasted_iota(jnp.int32, (n, n), 1)
    ends = jnp.dot(counts_b, upper.astype(F32).astype(BF16), preferred_element_type=F32)[:1]
    places = lax.broadcasted_iota(jnp.int32, (nrows, n), 0)
    below = ends <= places.astype(F32)
    owner_of = jnp.sum(jnp.where(below, 1.0, 0.0), axis=1, keepdims=True)
    start_of = jnp.max(jnp.where(below, ends, 0.0), axis=1, keepdims=True)
    slot_of = (owner_of * cap - start_of).astype(jnp.int32) + places[:, :1]
    hit = lax.broadcasted_iota(jnp.int32, (nrows, nslots), 1) == slot_of
    onehot_t[...] = hit.astype(F32).astype(BF16)
    cell_y = lax.div(cells_ref[...], nz)
    cell_z = lax.rem(cells_ref[...], nz)
    at_z = lax.broadcasted_iota(jnp.int32, (nz, nslots), 0) == cell_z
    paint_b[...] = at_z.astype(F32).astype(BF16)
    acc[...] = jnp.zeros_like(acc)
    sgt[...] = jnp.zeros_like(sgt)

    waits(send, arr, a2a_sem, n - 1).wait_recv()

    arrived = arr[...].reshape(nslots, feats)
    projected = lax.dot_general(
        wp_ref[...], arrived, (((0,), (1,)), ((), ())), preferred_element_type=F32
    )
    projected = projected.astype(BF16).astype(F32)
    for y in range(cy):
        paint_a[y] = jnp.where(cell_y == y, projected, 0.0).astype(BF16)

    def edge_copy(buf, row, side, b, send_sems, recv_sems):
        to_y = lax.rem(gj + (1 if side == 0 else ngy - 1), ngy)
        to_x = lax.rem(gi + b + ngx, ngx)
        return pltpu.make_async_remote_copy(
            src_ref=buf.at[row, 1],
            dst_ref=buf.at[0 if side == 0 else cy + 1, 1 - b],
            send_sem=send_sems.at[side, 1 - b],
            recv_sem=recv_sems.at[side, 1 - b],
            device_id=(to_x, to_y),
            device_id_type=MESH,
        )

    def plane_copy(buf, c, first, count, b, send_sems, recv_sems):
        to_x = lax.rem(gi + b + ngx, ngx)
        rows = pl.ds(first + 1, count)
        return pltpu.make_async_remote_copy(
            src_ref=buf.at[rows, 1],
            dst_ref=buf.at[rows, 1 - b],
            send_sem=send_sems.at[c, (1 - b) // 2],
            recv_sem=recv_sems.at[c, (1 - b) // 2],
            device_id=(to_x, gj),
            device_id_type=MESH,
        )

    f_planes = [
        [plane_copy(fld, c, first, count, b, fx_send, fx_recv) for b in (-1, 1)]
        for c, (first, count) in enumerate(F_CHUNKS)
    ]
    g_planes = [
        [plane_copy(pgr, c, first, count, b, gx_send, gx_recv) for b in (-1, 1)]
        for c, (first, count) in enumerate(F_ROWS)
    ]
    f_edges = [
        [edge_copy(fld, row, side, b, fy_send, fy_recv) for b in (-1, 0, 1)]
        for side, row in ((0, cy), (1, 1))
    ]
    g_edges = [
        [edge_copy(pgr, row, side, b, gy_send, gy_recv) for b in (-1, 0, 1)]
        for side, row in ((0, cy), (1, 1))
    ]

    for c, (first, count) in enumerate(F_CHUNKS):
        rows = slice(first, first + count)
        painted = nt_dot(paint_a[rows].reshape(count * chans, nslots), paint_b[...])
        painted = painted.reshape(count, chans, nz)
        fld[first + 1 : first + count + 1, 1] = (base_ref[rows].astype(F32) + painted).astype(BF16)
        if first == 0:
            for copy in f_edges[1]:
                copy.start()
        if first + count == cy:
            for copy in f_edges[0]:
                copy.start()
        for copy in f_planes[c]:
            copy.start()

    def forward_row(y, _):
        slab = fld[pl.ds(y, 3)].reshape(N_TAPS * chans, nz)
        part = jnp.dot(wf_ref[...], slab, preferred_element_type=F32)
        pre = roll_z(part[:chans], 1) + part[chans : 2 * chans] + roll_z(part[2 * chans :], -1)
        sig = jax.nn.sigmoid(pre)
        out_ref[y] = (fld[y + 1, 1].astype(F32) + pre * sig).astype(BF16)
        grad = cot_ref[y].astype(F32) * sig * (1.0 + pre * (1.0 - sig))
        grad = grad.astype(BF16)
        pgr[y + 1, 1] = grad
        wide = grad.astype(F32)
        three = jnp.concatenate([roll_z(wide, -1), wide, roll_z(wide, 1)], axis=0)
        acc[:, : N_TAPS * chans] += nt_dot(three.astype(BF16), slab)
        return 0

    for c, (first, count) in enumerate(F_ROWS):
        for copy in f_planes[c]:
            copy.wait_recv()
        if c < 2:
            for copy in f_edges[c]:
                copy.wait_recv()
        lax.fori_loop(first, first + count, forward_row, 0)
        if first == 0:
            for copy in g_edges[1]:
                copy.start()
        if first + count == cy:
            for copy in g_edges[0]:
                copy.start()
        for copy in g_planes[c]:
            copy.start()

    per_row = acc.shape[1] // 128
    for t in range(120):
        r, q = divmod(t, per_row)
        tiles[t // per, t % per] = acc[8 * r : 8 * r + 8, 128 * q : 128 * q + 128]

    def scatter(lo, hi, s):
        @pl.loop(1, n)
        def _(k):
            peer = peer_of(k)

            @pl.when((peer >= lo) & (peer < hi))
            def _():
                pltpu.make_async_remote_copy(
                    src_ref=tiles.at[peer],
                    dst_ref=rs.at[me],
                    send_sem=rs_sem.at[s, 0],
                    recv_sem=rs_sem.at[s, 1],
                    device_id=coords(peer),
                    device_id_type=MESH,
                ).start()

    def reduce_gather(lo, hi, s):
        @pl.when((me >= lo) & (me < hi))
        def _():
            waits(tiles, rs, rs_sem.at[s], n - 1).wait_recv()
            rs[pl.ds(me, 1)] = tiles[pl.ds(me, 1)]
            ag[pl.ds(me, 1)] = jnp.sum(rs[...], axis=0, keepdims=True)

            @pl.loop(1, n)
            def _(k):
                pltpu.make_async_remote_copy(
                    src_ref=ag.at[me],
                    dst_ref=ag.at[me],
                    send_sem=ag_sem.at[s, 0],
                    recv_sem=ag_sem.at[s, 1],
                    device_id=coords(peer_of(k)),
                    device_id_type=MESH,
                ).start()

    def finish(lo, hi, s):
        own = (me >= lo) & (me < hi)

        @pl.when(own)
        def _():
            waits(tiles, rs, ag_sem.at[s], n - 1).wait_send()
            if hi - lo > 1:
                waits(tiles, ag, rs_sem.at[s], hi - lo - 1).wait_send()
                waits(tiles, ag, ag_sem.at[s], hi - lo - 1).wait_recv()

        @pl.when(jnp.logical_not(own))
        def _():
            waits(tiles, ag, rs_sem.at[s], hi - lo).wait_send()
            waits(tiles, ag, ag_sem.at[s], hi - lo).wait_recv()

    scatter(0, nconv, 0)

    def backward_row(y, _):
        slab = pgr[pl.ds(y, 3)].reshape(N_TAPS * chans, nz)
        part = jnp.dot(wb_ref[...], slab, preferred_element_type=F32)
        got = roll_z(part[:chans], 1) + part[chans : 2 * chans] + roll_z(part[2 * chans :], -1)
        fg[y] = (cot_ref[y].astype(F32) + got).astype(BF16)
        return 0

    for c, (first, count) in enumerate(G_ROWS):
        for copy in g_planes[c]:
            copy.wait_recv()
        if c < 2:
            for copy in g_edges[c]:
                copy.wait_recv()
        lax.fori_loop(first, first + count, backward_row, 0)
        rows = fg[first : first + count].reshape(count * chans, nz)
        at_slots = jnp.dot(rows, paint_b[...], preferred_element_type=F32)
        total = sgt[:chans]
        for y in range(count):
            part = at_slots[y * chans : (y + 1) * chans]
            total = total + jnp.where(cell_y == first + y, part, 0.0)
        sgt[:chans] = total

    sgs[...] = sgt[...].T.astype(BF16).reshape(sgs.shape)
    spread(sgs, sgr, rev_sem)
    proj_part = jnp.dot(sgt[:chans].astype(BF16), arrived, preferred_element_type=F32)
    for r in range(chans // 8):
        t = 120 + r
        tiles[t // per, t % per] = proj_part[8 * r : 8 * r + 8]
    scatter(nconv, n, 1)
    reduce_gather(0, nconv, 0)
    waits(sgs, sgr, rev_sem, n - 1).wait_recv()
    back = sgr[...].reshape(nslots, feats)
    row_slot_grads = jnp.dot(onehot_t[...], back, preferred_element_type=F32).astype(BF16)
    rowg_ref[...] = jnp.dot(row_slot_grads, wpt_ref[...], preferred_element_type=F32)
    reduce_gather(nconv, n, 1)
    finish(0, nconv, 0)
    for t in range(120):
        r, q = divmod(t, per_row)
        acc[8 * r : 8 * r + 8, 128 * q : 128 * q + 128] = ag[t // per, t % per]
    conv_scale = 1.0 / math.sqrt(cy * nz * n)
    for x in range(3):
        for y in range(3):
            for z in range(3):
                at = (y * 3 + x) * chans
                block = acc[z * chans : (z + 1) * chans, at : at + chans]
                convg_ref[x * 9 + y * 3 + z] = block * conv_scale
    finish(nconv, n, 1)
    proj_scale = 1.0 / math.sqrt(nrows * n)
    for r in range(chans // 8):
        t = 120 + r
        projg_ref[8 * r : 8 * r + 8] = ag[t // per, t % per] * proj_scale

    waits(send, arr, a2a_sem, n - 1).wait_send()
    waits(sgs, sgr, rev_sem, n - 1).wait_send()
    for group in (f_planes, g_planes, f_edges, g_edges):
        for copies in group:
            for copy in copies:
                copy.wait_send()


def local(ngx, ngy, particles, send_counts, cell_lists, base_field, proj_weight, conv_weight, cotangent):
    n = ngx * ngy
    nrows, feats = particles.shape
    chans, _, cy, nz = base_field.shape
    nslots = cell_lists.shape[1]
    base = base_field.reshape(chans, cy, nz).transpose(1, 0, 2)
    cot = cotangent.reshape(chans, cy, nz).transpose(1, 0, 2)
    taps = conv_weight.reshape(3, 3, 3, chans, chans)
    wf = taps.transpose(2, 3, 1, 0, 4).reshape(3 * chans, N_TAPS * chans)
    wb = taps[::-1, ::-1, ::-1].transpose(2, 4, 1, 0, 3).reshape(3 * chans, N_TAPS * chans)
    wpt = jnp.pad(proj_weight.T, ((0, feats - chans), (0, 0)))
    per = 128 // n
    dma = pltpu.SemaphoreType.DMA
    vmem = pl.BlockSpec(memory_space=pltpu.VMEM)
    out, rowg, convg, projg = pl.pallas_call(
        functools.partial(kernel, ngx, ngy),
        out_shape=(
            jax.ShapeDtypeStruct((cy, chans, nz), BF16),
            jax.ShapeDtypeStruct((nrows, feats), F32),
            jax.ShapeDtypeStruct((27, chans, chans), F32),
            jax.ShapeDtypeStruct((chans, feats), F32),
        ),
        in_specs=[vmem] * 9,
        out_specs=[vmem] * 4,
        scratch_shapes=[
            pltpu.VMEM((n, nslots // n, feats), BF16),
            pltpu.VMEM((n, nslots // n, feats), BF16),
            pltpu.VMEM((nrows, nslots), BF16),
            pltpu.VMEM((cy, chans, nslots), BF16),
            pltpu.VMEM((nz, nslots), BF16),
            pltpu.VMEM((cy + 2, 3, chans, nz), BF16),
            pltpu.VMEM((cy + 2, 3, chans, nz), BF16),
            pltpu.VMEM((cy, chans, nz), BF16),
            pltpu.VMEM((feats, nslots), F32),
            pltpu.VMEM((3 * chans, 640), F32),
            pltpu.VMEM((n, per, 8, 128), F32),
            pltpu.VMEM((n, per, 8, 128), F32),
            pltpu.VMEM((n, per, 8, 128), F32),
            pltpu.VMEM((n, nslots // n, feats), BF16),
            pltpu.VMEM((n, nslots // n, feats), BF16),
            dma((2,)),
            dma((2,)),
            dma((2, 2)),
            dma((2, 2)),
            dma((4, 2)),
            dma((4, 2)),
            dma((2, 3)),
            dma((2, 3)),
            dma((4, 2)),
            dma((4, 2)),
            dma((2, 3)),
            dma((2, 3)),
        ],
        compiler_params=pltpu.CompilerParams(
            collective_id=0, has_side_effects=True, vmem_limit_bytes=56 * 1024 * 1024
        ),
        name="section",
    )(send_counts, cell_lists, particles, base, cot, wf, wb, proj_weight, wpt)
    out_field = out.transpose(1, 0, 2).reshape(chans, 1, cy, nz)
    return out_field, rowg, convg, projg.T


def solution(mesh):
    in_specs = (
        P(("gx", "gy"), None),
        P(("gx", "gy"), None),
        P(("gx", "gy"), None),
        P(None, "gx", "gy", None),
        P(),
        P(),
        P(None, "gx", "gy", None),
    )
    out_specs = (P(None, "gx", "gy", None), P(("gx", "gy"), None), P(), P())
    body = functools.partial(local, mesh.shape["gx"], mesh.shape["gy"])
    return jax.shard_map(body, mesh=mesh, in_specs=in_specs, out_specs=out_specs, check_vma=False)
```

profile of v0, /device:TPU:1, one launch (start us, length us, event | category | flops | bytes accessed | tf_op | source)
XLA Modules:
  0.0 110.5 jit_solution(5956712089938244290)
XLA Ops:
  0.6 0.0 copy-start.4
  0.6 1.4 %pad.4.wpt_ref = bf16[128,128]{1,0:T(8,128)(2,1)} pad(bf16[64,128]{1,0:T(8,128)(2,1)} %bitcast.23, bf16[]{:T(256)} %constant.2.clone.1), padding=0_64x0_0 | pad | bytes 49154 | tf_op jit(solution)/shard_map/jit(_pad)/pad | solution.py:376
  2.0 0.0 copy-done.4
  2.0 0.7 copy.21.wp_ref
  2.8 1.6 %copy.20 = bf16[3,3,3,64,64]{3,0,1,4,2:T(4,128)(2,1)S(1)} copy(bf16[3,3,3,64,64]{4,3,2,1,0:T(8,128)(2,1)} %bitcast.20) | data formatting | bytes 442368 | tf_op jit(solution)/shard_map/reshape | solution.py:373
  4.4 2.4 %rev.3 = bf16[3,3,3,64,64]{3,0,1,4,2:T(4,128)(2,1)S(1)} reverse(bf16[3,3,3,64,64]{3,0,1,4,2:T(4,128)(2,1)S(1)} %copy.20), dimensions={0,1,2} | reverse | bytes 442368 | tf_op jit(solution)/shard_map/rev | solution.py:375
  6.8 0.0 copy-start
  6.8 1.1 %reshape.30.wb_ref = bf16[192,576]{1,0:T(8,128)(2,1)} reshape(bf16[3,64,3,3,64]{4,3,2,1,0:T(4,128)(2,1)S(1)} %bitcast.18) | data formatting | bytes 442368 | tf_op jit(solution)/shard_map/reshape | solution.py:375
  7.9 0.0 copy-done
  7.9 0.0 copy-start.3
  7.9 0.4 copy.26
  8.3 0.0 copy-start.2
  8.3 1.1 reshape.29.wf_ref
  9.4 0.0 copy-done.3
  9.4 0.0 copy-done.2
  9.4 1.3 %copy_bitcast_fusion.1 = (bf16[16,64,256]{2,1,0:T(8,128)(2,1)}, bf16[16,64,256]{2,1,0:T(8,128)(2,1)}) fusion(bf16[64,1,16,256]{3,2,1,0:T(8,128)(2,1)S(1)} %copy-done.2, bf16[64,1,16,256]{3,2,1,0:T(8,128)(2,1)S(1)} %copy-done.3), kind=kLoop, calls=%fused_computation.1 | loop fusion | bytes 2097152 | tf_op jit(solution)/shard_map/transpose | solution.py:372
  10.7 94.4 %section.1 = (bf16[16,64,256]{2,1,0:T(8,128)(2,1)}, f32[512,128]{1,0:T(8,128)}, f32[27,64,64]{2,1,0:T(8,128)}, f32[64,128]{1,0:T(8,128)}) custom-call(s32[1,128]{1,0:T(1,128)} %counts_ref.1, s32[1,1024]{1,0:T(1,128)} %cells_ref.1, bf16[512,128]{1,0:T(8,128)(2,1)} %rows_ref.1, bf16[16,64,256]{2,1,0:T(8,128)(2,1)} %get-tuple-element.21.base_ref, ...), custom_call_target="tpu_custom_call" | custom-call | tf_op jit(solution)/shard_map/section/pallas_call | solution.py:380
  105.1 0.0 copy-start.1
  105.1 2.2 %copy.22 = bf16[64,1,16,256]{3,2,1,0:T(8,128)(2,1)} copy(bf16[64,1,16,256]{3,0,2,1:T(8,128)(2,1)} %bitcast.22) | data formatting | bytes 1048576
  107.3 1.7 %copy.30 = f32[512,128]{1,0:T(8,128)} copy(f32[512,128]{1,0:T(8,128)} %get-tuple-element.27) | data formatting | bytes 524288
  109.0 0.0 copy-done.1
  109.0 0.0 copy-start.5
  109.0 0.9 copy.31
  109.9 0.0 copy-done.5
  109.9 0.6 copy.32
Async XLA Ops:
  0.6 1.4 %copy-start.4 = (bf16[128,64]{0,1:T(8,128)(2,1)S(1)}, bf16[128,64]{0,1:T(8,128)(2,1)}, u32[]{:S(2)}) copy-start(bf16[128,64]{0,1:T(8,128)(2,1)} %param.11) | copy-start | bytes 49156
  6.8 1.1 %copy-start = (bf16[27,64,64]{2,1,0:T(8,128)(2,1)S(1)}, bf16[27,64,64]{2,1,0:T(8,128)(2,1)}, u32[]{:S(2)}) copy-start(bf16[27,64,64]{2,1,0:T(8,128)(2,1)} %param.12) | copy-start | bytes 663556
  7.9 1.5 %copy-start.3 = (bf16[64,1,16,256]{3,2,1,0:T(8,128)(2,1)S(1)}, bf16[64,1,16,256]{3,2,1,0:T(8,128)(2,1)}, u32[]{:S(2)}) copy-start(bf16[64,1,16,256]{3,2,1,0:T(8,128)(2,1)} %param.10) | copy-start | bytes 1572868
  8.3 1.1 %copy-start.2 = (bf16[64,1,16,256]{3,2,1,0:T(8,128)(2,1)S(1)}, bf16[64,1,16,256]{3,2,1,0:T(8,128)(2,1)}, u32[]{:S(2)}) copy-start(bf16[64,1,16,256]{3,2,1,0:T(8,128)(2,1)} %param.13) | copy-start | bytes 1572868
  105.1 3.9 %copy-start.1 = (f32[27,64,64]{2,1,0:T(8,128)S(1)}, f32[27,64,64]{2,1,0:T(8,128)}, u32[]{:S(2)}) copy-start(f32[27,64,64]{2,1,0:T(8,128)} %get-tuple-element.28) | copy-start | bytes 1327108
  109.0 0.9 copy-start.5
where the time goes:
time: 112 us; the launch traced here: 111 us
  Pallas kernels  94.4 us (84%)
  local copies, waits for them, and re-layouts  15.4 us (14%)
    pallas_call x1, Pallas kernels, local(): pl.pallas_call(functools.partial(kernel, ngx, ngy), out_shape=(jax.ShapeD...  94.4 us
    unnamed x17, local copies, waits for them, and re-layouts  6.15 us
    rev x1, local copies, waits for them, and re-layouts, local(): taps[::-1, ::-1, ::-1].transpose(2, 4, 1, 0, 3)  2.35 us

commit v1 on v0

v1 whole, which is shorter than its diff:
```python
import functools
import math

import jax
import jax.numpy as jnp
from jax import lax
from jax.experimental import pallas as pl
from jax.experimental.pallas import tpu as pltpu
from jax.sharding import PartitionSpec as P

MESH = pl.DeviceIdType.MESH
F32 = jnp.float32
BF16 = jnp.bfloat16

F_CHUNKS = ((0, 4), (12, 4), (4, 4), (8, 4))
F_ROWS = ((0, 3), (13, 3), (3, 4), (7, 6))
N_TAPS = 9


def nt_dot(a, b):
    return lax.dot_general(a, b, (((1,), (1,)), ((), ())), preferred_element_type=F32)


def roll_z(x, shift):
    return pltpu.roll(x, shift % x.shape[1], 1)


def kernel(
    ngx,
    ngy,
    counts_ref,
    cells_ref,
    rows_ref,
    base_ref,
    cot_ref,
    taps_ref,
    wpt_ref,
    out_ref,
    back_ref,
    sums_ref,
    psum_ref,
    send,
    arr,
    paint_a,
    paint_b,
    perm,
    perm_back,
    wf,
    wb,
    base,
    cot,
    outs,
    fld,
    pgr,
    grads,
    near_cells,
    near_out,
    near_in,
    acc,
    tiles,
    rs,
    ag,
    ptiles,
    prs,
    pag,
    sgs,
    sgr,
    a2a_sem,
    rev_sem,
    cell_sem,
    near_sem,
    rs_sem,
    ag_sem,
    prs_sem,
    pag_sem,
    fx_send,
    fx_recv,
    fy_send,
    fy_recv,
    gy_send,
    gy_recv,
):
    n = ngx * ngy
    nrows, feats = rows_ref.shape
    cy, chans, nz = base.shape
    nslots = cells_ref.shape[1]
    cap = nslots // n
    per = tiles.shape[1]
    nconv = 120 // per
    gi = lax.axis_index("gx")
    gj = lax.axis_index("gy")
    me = gi * ngy + gj

    def coords(d):
        return (lax.div(d, ngy), lax.rem(d, ngy))

    def peer_of(k):
        return lax.rem(me + k, n)

    def beside(b):
        return (lax.rem(gi + b + ngx, ngx), gj)

    barrier = pltpu.get_barrier_semaphore()

    @pl.loop(1, n)
    def _(k):
        pl.semaphore_signal(barrier, inc=1, device_id=coords(peer_of(k)), device_id_type=MESH)

    counts = counts_ref[...].astype(F32)
    lane = lax.broadcasted_iota(jnp.int32, (nslots, n), 1)
    slot = lax.broadcasted_iota(jnp.int32, (nslots, 1), 0)
    owner = slot // cap
    offs = jnp.sum(jnp.where(lane < owner, counts, 0.0), axis=1, keepdims=True)
    mine = jnp.sum(jnp.where(lane == owner, counts, 0.0), axis=1, keepdims=True)
    place = slot - owner * cap
    index = jnp.where(place < mine.astype(jnp.int32), offs.astype(jnp.int32) + place, -1)
    pick = lax.broadcasted_iota(jnp.int32, (nslots, nrows), 1) == index
    outgoing = jnp.dot(pick.astype(F32).astype(BF16), rows_ref[...], preferred_element_type=F32)
    send[...] = outgoing.astype(BF16).reshape(send.shape)

    pl.semaphore_wait(barrier, n - 1)

    def remote(src, dst, send_sem, recv_sem, device):
        return pltpu.make_async_remote_copy(
            src_ref=src,
            dst_ref=dst,
            send_sem=send_sem,
            recv_sem=recv_sem,
            device_id=device,
            device_id_type=MESH,
        )

    def spread(src, dst, sems):
        @pl.loop(1, n)
        def _(k):
            peer = peer_of(k)
            remote(src.at[peer], dst.at[me], sems.at[0], sems.at[1], coords(peer)).start()

        dst[pl.ds(me, 1)] = src[pl.ds(me, 1)]

    def waits(src, dst, sems, count):
        part = pl.ds(0, count)
        return remote(src.at[part], dst.at[part], sems.at[0], sems.at[1], coords(peer_of(1)))

    spread(send, arr, a2a_sem)
    cell_copies = [
        remote(
            cells_ref,
            near_cells.at[(1 - b) // 2],
            cell_sem.at[0, (1 - b) // 2],
            cell_sem.at[1, (1 - b) // 2],
            beside(b),
        )
        for b in (-1, 1)
    ]
    for copy in cell_copies:
        copy.start()

    def at_depth(cells):
        hit = lax.broadcasted_iota(jnp.int32, (nz, nslots), 0) == cells % nz
        return hit.astype(F32).astype(BF16)

    cell_y = cells_ref[...] // nz
    paint_b[0] = at_depth(cells_ref[...])
    full = cy * chans
    row = lax.broadcasted_iota(jnp.int32, (full, 1), 0)
    col = lax.broadcasted_iota(jnp.int32, (full, full), 1)
    perm[...] = (col == (row % chans) * cy + row // chans).astype(F32).astype(BF16)
    base[...] = (
        jnp.dot(perm[...], base_ref[...], preferred_element_type=F32).astype(BF16).reshape(base.shape)
    )
    cot[...] = (
        jnp.dot(perm[...], cot_ref[...], preferred_element_type=F32).astype(BF16).reshape(cot.shape)
    )
    for x in range(3):
        for y in range(3):
            for z in range(3):
                tap = taps_ref[x * 9 + y * 3 + z]
                at = (y * 3 + x) * chans
                wf[z * chans : (z + 1) * chans, at : at + chans] = tap
                at = (x * 3 + 2 - z) * chans
                side = (2 - y) * chans
                wb[at : at + chans, side : side + chans] = tap.astype(F32).T.astype(BF16)
    acc[...] = jnp.zeros_like(acc)

    waits(send, arr, a2a_sem, n - 1).wait_recv()

    arrived = arr[...].reshape(nslots, feats)
    projected = nt_dot(wpt_ref[...], arrived).astype(BF16).astype(F32)
    for y in range(cy):
        paint_a[y] = jnp.where(cell_y == y, projected, 0.0).astype(BF16)

    def edge_copy(side, b):
        to = (lax.rem(gi + b + ngx, ngx), lax.rem(gj + (1 if side == 0 else ngy - 1), ngy))
        row = cy if side == 0 else 1
        dst = 0 if side == 0 else cy + 1
        sem = (side, 1 - b)
        return remote(fld.at[row, 1], fld.at[dst, 1 - b], fy_send.at[sem], fy_recv.at[sem], to)

    def grad_edge(side):
        to = (gi, lax.rem(gj + (1 if side == 0 else ngy - 1), ngy))
        row = cy if side == 0 else 1
        dst = 0 if side == 0 else cy + 1
        return remote(pgr.at[row], pgr.at[dst], gy_send.at[side], gy_recv.at[side], to)

    def plane_copy(c, first, count, b):
        rows = pl.ds(first + 1, count)
        sem = (c, (1 - b) // 2)
        return remote(
            fld.at[rows, 1], fld.at[rows, 1 - b], fx_send.at[sem], fx_recv.at[sem], beside(b)
        )

    f_planes = [
        [plane_copy(c, first, count, b) for b in (-1, 1)]
        for c, (first, count) in enumerate(F_CHUNKS)
    ]
    f_edges = [[edge_copy(side, b) for b in (-1, 0, 1)] for side in (0, 1)]
    g_edges = [grad_edge(side) for side in (0, 1)]

    for c, (first, count) in enumerate(F_CHUNKS):
        rows = slice(first, first + count)
        painted = nt_dot(paint_a[rows].reshape(count * chans, nslots), paint_b[0])
        painted = painted.reshape(count, chans, nz)
        fld[first + 1 : first + count + 1, 1] = (base[rows].astype(F32) + painted).astype(BF16)
        if first == 0:
            for copy in f_edges[1]:
                copy.start()
        if first + count == cy:
            for copy in f_edges[0]:
                copy.start()
        if c < 2:
            for copy in f_planes[c]:
                copy.start()

    for copy in cell_copies:
        copy.wait()
    near_y = [near_cells[e] // nz for e in (0, 1)]
    for e in (0, 1):
        paint_b[1 + e] = at_depth(near_cells[e])

    for c, (first, count) in enumerate(F_ROWS):
        for copy in f_planes[c]:
            copy.wait()
        if c + 2 < len(F_CHUNKS):
            for copy in f_planes[c + 2]:
                copy.start()
        if c < 2:
            for copy in f_edges[c]:
                copy.wait_recv()
        slabs, threes = [], []
        for y in range(first, first + count):
            slab = fld[y : y + 3].reshape(N_TAPS * chans, nz)
            part = jnp.dot(wf[...], slab, preferred_element_type=F32)
            pre = roll_z(part[:chans], 1) + part[chans : 2 * chans] + roll_z(part[2 * chans :], -1)
            sig = jax.nn.sigmoid(pre)
            outs[y] = (fld[y + 1, 1].astype(F32) + pre * sig).astype(BF16)
            grad = (cot[y].astype(F32) * sig * (1.0 + pre * (1.0 - sig))).astype(BF16)
            pgr[y + 1] = grad
            wide = grad.astype(F32)
            three = jnp.concatenate([roll_z(wide, -1), wide, roll_z(wide, 1)], axis=0)
            slabs.append(slab)
            threes.append(three.astype(BF16))
        if c < 2:
            g_edges[1 - c].start()
        acc[:, : N_TAPS * chans] += nt_dot(
            jnp.concatenate(threes, axis=1), jnp.concatenate(slabs, axis=1)
        )

    per_row = acc.shape[1] // 128
    for t in range(120):
        r, q = divmod(t, per_row)
        tiles[t // per, t % per] = acc[8 * r : 8 * r + 8, 128 * q : 128 * q + 128]

    def scatter(src, dst, sems, count, step):
        @pl.loop(1, n)
        def _(k):
            peer = peer_of(k)
            share = lax.div(peer, step)

            @pl.when((share < count) & (share * step == peer))
            def _():
                remote(src.at[share], dst.at[me], sems.at[0], sems.at[1], coords(peer)).start()

    def mine_of(count, step):
        share = lax.div(me, step)
        return share, (share < count) & (share * step == me)

    def reduce_gather(src, part, dst, sems, gather_sems, count, step):
        share, own = mine_of(count, step)

        @pl.when(own)
        def _():
            waits(part, part, sems, n - 1).wait_recv()
            part[pl.ds(me, 1)] = src[pl.ds(share, 1)]
            dst[pl.ds(share, 1)] = jnp.sum(part[...], axis=0, keepdims=True)

            @pl.loop(1, n)
            def _(k):
                there = dst.at[share]
                remote(
                    there, there, gather_sems.at[0], gather_sems.at[1], coords(peer_of(k))
                ).start()

    def finish(part, dst, sems, gather_sems, count, step):
        _, own = mine_of(count, step)

        @pl.when(own)
        def _():
            waits(part, part, gather_sems, n - 1).wait_send()
            if count > 1:
                waits(dst, dst, sems, count - 1).wait_send()
                waits(dst, dst, gather_sems, count - 1).wait_recv()

        @pl.when(jnp.logical_not(own))
        def _():
            waits(dst, dst, sems, count).wait_send()
            waits(dst, dst, gather_sems, count).wait_recv()

    scatter(tiles, rs, rs_sem, nconv, 1)

    for c, (first, count) in enumerate(((1, cy - 2), (0, 1), (cy - 1, 1))):
        if c == 1:
            for copy in g_edges:
                copy.wait_recv()
        for y in range(first, first + count):
            slab = pgr[y : y + 3].reshape(3 * chans, nz)
            part = jnp.dot(wb[...], slab, preferred_element_type=F32)
            for x in range(3):
                p = part[3 * x * chans : 3 * (x + 1) * chans]
                got = roll_z(p[:chans], 1) + p[chans : 2 * chans] + roll_z(p[2 * chans :], -1)
                if x == 1:
                    got = got + cot[y].astype(F32)
                    high = got.astype(BF16)
                    grads[3, y] = (got - high.astype(F32)).astype(BF16)
                    grads[1, y] = high
                else:
                    grads[x, y] = got.astype(BF16)

    def at_slots(which, depth, ys, total):
        step = 4
        for first in range(0, cy, step):
            rows = grads[which, first : first + step].reshape(step * chans, nz)
            got = jnp.dot(rows, paint_b[depth], preferred_element_type=F32)
            for y in range(step):
                part = got[y * chans : (y + 1) * chans]
                total = total + jnp.where(ys == first + y, part, 0.0)
        return total

    zero = jnp.zeros((chans, nslots), F32)
    near_copies = []
    for e, b in ((0, -1), (1, 1)):
        near_out[e] = at_slots(1 + b, 1 + e, near_y[e], zero).astype(BF16)
        copy = remote(
            near_out.at[e], near_in.at[1 - e], near_sem.at[0, e], near_sem.at[1, 1 - e], beside(b)
        )
        copy.start()
        near_copies.append(copy)
    slot_grad = at_slots(1, 0, cell_y, at_slots(3, 0, cell_y, zero))
    reduce_gather(tiles, rs, ag, rs_sem, ag_sem, nconv, 1)
    for copy in near_copies:
        copy.wait()
    slot_grad = slot_grad + near_in[0].astype(F32) + near_in[1].astype(F32)

    slot_grad = slot_grad.astype(BF16)
    wide = jnp.concatenate([slot_grad.astype(F32), jnp.zeros((feats - chans, nslots), F32)], axis=0)
    sgs[...] = wide.T.astype(BF16).reshape(sgs.shape)
    spread(sgs, sgr, rev_sem)
    proj_part = jnp.dot(slot_grad, arrived, preferred_element_type=F32)
    ptiles[...] = proj_part.reshape(ptiles.shape)
    step = n // min(n, chans)
    pcount = ptiles.shape[0]
    scatter(ptiles, prs, prs_sem, pcount, step)

    row = lax.broadcasted_iota(jnp.int32, (full, 1), 0)
    perm_back[...] = (col == (row % cy) * chans + row // cy).astype(F32).astype(BF16)
    out_ref[...] = jnp.dot(
        perm_back[...], outs[...].reshape(full, nz), preferred_element_type=F32
    ).astype(BF16)

    reduce_gather(ptiles, prs, pag, prs_sem, pag_sem, pcount, step)
    waits(sgs, sgr, rev_sem, n - 1).wait_recv()
    back_ref[...] = sgr[...].reshape(nslots, feats)
    finish(rs, ag, rs_sem, ag_sem, nconv, 1)
    sums_ref[...] = ag[:nconv]
    finish(prs, pag, prs_sem, pag_sem, pcount, step)
    psum_ref[...] = pag[...].reshape(psum_ref.shape)

    waits(send, arr, a2a_sem, n - 1).wait_send()
    waits(sgs, sgr, rev_sem, n - 1).wait_send()
    for copies in f_edges:
        for copy in copies:
            copy.wait_send()
    for copy in g_edges:
        copy.wait_send()


def ending(
    count_all, counts_ref, back_ref, sums_ref, psum_ref, outf_ref, wpt_ref, out_ref, rowg_ref, convg_ref, projg_ref
):
    n = counts_ref.shape[1]
    nslots, feats = back_ref.shape
    chans = wpt_ref.shape[0]
    nrows = rowg_ref.shape[0]
    cap = nslots // n
    out_ref[...] = outf_ref[...]
    counts = jnp.broadcast_to(counts_ref[...].astype(F32), (8, n)).astype(BF16)
    upper = lax.broadcasted_iota(jnp.int32, (n, n), 0) <= lax.broadcasted_iota(jnp.int32, (n, n), 1)
    ends = jnp.dot(counts, upper.astype(F32).astype(BF16), preferred_element_type=F32)[:1]
    places = lax.broadcasted_iota(jnp.int32, (nrows, 1), 0)
    below = ends <= places.astype(F32)
    owner_of = jnp.sum(jnp.where(below, 1.0, 0.0), axis=1, keepdims=True)
    start_of = jnp.max(jnp.where(below, ends, 0.0), axis=1, keepdims=True)
    slot_of = (owner_of * cap - start_of).astype(jnp.int32) + places
    hit = lax.broadcasted_iota(jnp.int32, (nrows, nslots), 1) == slot_of
    back = jnp.dot(hit.astype(F32).astype(BF16), back_ref[...], preferred_element_type=F32)
    rowg_ref[...] = jnp.dot(
        back[:, :chans].astype(BF16), wpt_ref[...], preferred_element_type=F32
    )
    per = sums_ref.shape[1]
    rows = []
    for r in range(3 * chans // 8):
        tiles = [sums_ref[t // per, t % per] for t in range(5 * r, 5 * r + 5)]
        rows.append(jnp.concatenate(tiles, axis=1))
    sums = jnp.concatenate(rows, axis=0) * (1.0 / math.sqrt(count_all))
    for x in range(3):
        for y in range(3):
            for z in range(3):
                at = (y * 3 + x) * chans
                convg_ref[x * 9 + y * 3 + z] = sums[z * chans : (z + 1) * chans, at : at + chans]
    projg_ref[...] = psum_ref[...] * (1.0 / math.sqrt(nrows * n))


def local(ngx, ngy, particles, send_counts, cell_lists, base_field, proj_weight, conv_weight, cotangent):
    n = ngx * ngy
    nrows, feats = particles.shape
    chans, _, cy, nz = base_field.shape
    nslots = cell_lists.shape[1]
    full = chans * cy
    cap = nslots // n
    per = 128 // n
    pcount = min(n, chans)
    prow = chans // pcount
    weight_t = proj_weight.T
    dma = pltpu.SemaphoreType.DMA
    vmem = pl.BlockSpec(memory_space=pltpu.VMEM)
    plane = (cy, chans, nz)
    out, back, sums, psum = pl.pallas_call(
        functools.partial(kernel, ngx, ngy),
        out_shape=(
            jax.ShapeDtypeStruct((full, nz), BF16),
            jax.ShapeDtypeStruct((nslots, feats), BF16),
            jax.ShapeDtypeStruct((120 // per, per, 8, 128), F32),
            jax.ShapeDtypeStruct((chans, feats), F32),
        ),
        in_specs=[vmem] * 7,
        out_specs=[vmem] * 4,
        scratch_shapes=[
            pltpu.VMEM((n, cap, feats), BF16),
            pltpu.VMEM((n, cap, feats), BF16),
            pltpu.VMEM((cy, chans, nslots), BF16),
            pltpu.VMEM((3, nz, nslots), BF16),
            pltpu.VMEM((full, full), BF16),
            pltpu.VMEM((full, full), BF16),
            pltpu.VMEM((3 * chans, N_TAPS * chans), BF16),
            pltpu.VMEM((N_TAPS * chans, 3 * chans), BF16),
            pltpu.VMEM(plane, BF16),
            pltpu.VMEM(plane, BF16),
            pltpu.VMEM(plane, BF16),
            pltpu.VMEM((cy + 2, 3, chans, nz), BF16),
            pltpu.VMEM((cy + 2, chans, nz), BF16),
            pltpu.VMEM((4, cy, chans, nz), BF16),
            pltpu.VMEM((2, 1, nslots), jnp.int32),
            pltpu.VMEM((2, chans, nslots), BF16),
            pltpu.VMEM((2, chans, nslots), BF16),
            pltpu.VMEM((3 * chans, 640), F32),
            pltpu.VMEM((n, per, 8, 128), F32),
            pltpu.VMEM((n, per, 8, 128), F32),
            pltpu.VMEM((n, per, 8, 128), F32),
            pltpu.VMEM((pcount, prow, feats), F32),
            pltpu.VMEM((n, prow, feats), F32),
            pltpu.VMEM((pcount, prow, feats), F32),
            pltpu.VMEM((n, cap, feats), BF16),
            pltpu.VMEM((n, cap, feats), BF16),
            dma((2,)),
            dma((2,)),
            dma((2, 2)),
            dma((2, 2)),
            dma((2,)),
            dma((2,)),
            dma((2,)),
            dma((2,)),
            dma((4, 2)),
            dma((4, 2)),
            dma((2, 3)),
            dma((2, 3)),
            dma((2,)),
            dma((2,)),
        ],
        compiler_params=pltpu.CompilerParams(
            collective_id=0, has_side_effects=True, vmem_limit_bytes=44 * 1024 * 1024
        ),
        name="section",
    )(
        send_counts,
        cell_lists,
        particles,
        base_field.reshape(full, nz),
        cotangent.reshape(full, nz),
        conv_weight,
        weight_t,
    )
    out_field, row_grads, conv_grad, proj_t = pl.pallas_call(
        functools.partial(ending, cy * nz * n),
        out_shape=(
            jax.ShapeDtypeStruct((full, nz), BF16),
            jax.ShapeDtypeStruct((nrows, feats), F32),
            jax.ShapeDtypeStruct((27, chans, chans), F32),
            jax.ShapeDtypeStruct((chans, feats), F32),
        ),
        in_specs=[vmem] * 6,
        out_specs=[vmem] * 4,
        compiler_params=pltpu.CompilerParams(vmem_limit_bytes=16 * 1024 * 1024),
        name="ending",
    )(send_counts, back, sums, psum, out, weight_t)
    return out_field.reshape(base_field.shape), row_grads, conv_grad, proj_t.T


def solution(mesh):
    in_specs = (
        P(("gx", "gy"), None),
        P(("gx", "gy"), None),
        P(("gx", "gy"), None),
        P(None, "gx", "gy", None),
        P(),
        P(),
        P(None, "gx", "gy", None),
    )
    out_specs = (P(None, "gx", "gy", None), P(("gx", "gy"), None), P(), P())
    body = functools.partial(local, mesh.shape["gx"], mesh.shape["gy"])
    return jax.shard_map(body, mesh=mesh, in_specs=in_specs, out_specs=out_specs, check_vma=False)
```

time: 112 us -> 82.7 us (0.74)
  Pallas kernels: 94.4 us -> 76.3 us
  local copies, waits for them, and re-layouts: 15.4 us -> 5.39 us
    pallas_call x1, Pallas kernels: 94.4 us -> 74.3 us  [local(): pl.pallas_call(functools.partial(kernel, ngx, ngy), out_shape=(jax.ShapeD...]
    reshape x4 -> x0, local copies, waits for them, and re-layouts: 4.22 us -> none  [the longest x2 2.02 us: local(): taps = conv_weight.reshape(3, 3, 3, chans, chans)]
    rev x1 -> x0, local copies, waits for them, and re-layouts: 2.35 us -> none  [local(): taps[::-1, ::-1, ::-1].transpose(2, 4, 1, 0, 3)]
    pallas_call x0 -> x1, Pallas kernels: none -> 2.01 us  [local(): pl.pallas_call(functools.partial(ending, cy * nz * n), out_shape=(jax.Sha...]
    pad x1 -> x0, local copies, waits for them, and re-layouts: 1.4 us -> none  [local(): wpt = jnp.pad(proj_weight.T, ((0, feats - chans), (0, 0)))]
    transpose x1 -> x0, local copies, waits for them, and re-layouts: 1.32 us -> none  [local(): cot = cotangent.reshape(chans, cy, nz).transpose(1, 0, 2)]
    unnamed x17 -> x14, local copies, waits for them, and re-layouts: 6.15 us -> 5.39 us
where the time goes in v1:
time: 82.7 us; the launch traced here: 82.3 us
  Pallas kernels  76.3 us (92%)
  local copies, waits for them, and re-layouts  5.39 us (7%)
    pallas_call x1, Pallas kernels, local(): pl.pallas_call(functools.partial(kernel, ngx, ngy), out_shape=(jax.ShapeD...  74.3 us
    unnamed x14, local copies, waits for them, and re-layouts  5.39 us
    pallas_call x1, Pallas kernels, local(): pl.pallas_call(functools.partial(ending, cy * nz * n), out_shape=(jax.Sha...  2.01 us

profile of v1, /device:TPU:1, one launch (start us, length us, event | category | flops | bytes accessed | tf_op | source)
XLA Modules:
  0.0 82.3 jit_solution(4195550835229417813)
XLA Ops:
  0.6 0.0 copy-start.5
  0.6 0.0 copy-start.6
  0.7 0.7 copy-done.5
  1.3 0.0 copy-done.6
  1.3 0.0 copy-start
  1.3 1.0 %copy-done = bf16[64,1,16,256]{3,2,1,0:T(8,128)(2,1)S(1)} copy-done((bf16[64,1,16,256]{3,2,1,0:T(8,128)(2,1)S(1)}, bf16[64,1,16,256]{3,2,1,0:T(8,128)(2,1)}, u32[]{:S(2)}) %copy-start) | copy-done | bytes 524312
  2.4 0.0 copy-start.1
  2.4 1.0 %copy-done.1 = bf16[64,1,16,256]{3,2,1,0:T(8,128)(2,1)S(1)} copy-done((bf16[64,1,16,256]{3,2,1,0:T(8,128)(2,1)S(1)}, bf16[64,1,16,256]{3,2,1,0:T(8,128)(2,1)}, u32[]{:S(2)}) %copy-start.1) | copy-done | bytes 524312
  3.4 0.0 copy-start.2
  3.4 1.0 %copy-done.2 = bf16[27,64,64]{2,1,0:T(8,128)(2,1)S(1)} copy-done((bf16[27,64,64]{2,1,0:T(8,128)(2,1)S(1)}, bf16[27,64,64]{2,1,0:T(8,128)(2,1)}, u32[]{:S(2)}) %copy-start.2) | copy-done | bytes 221208
  4.4 0.0 copy-start.3
  4.4 0.9 %copy-done.3 = bf16[512,128]{1,0:T(8,128)(2,1)S(1)} copy-done((bf16[512,128]{1,0:T(8,128)(2,1)S(1)}, bf16[512,128]{1,0:T(8,128)(2,1)}, u32[]{:S(2)}) %copy-start.3) | copy-done | bytes 131096
  5.3 0.0 copy-start.4
  5.3 0.7 copy-done.4
  6.0 74.3 %section.1 = (bf16[1024,256]{1,0:T(8,128)(2,1)S(1)}, bf16[1024,128]{1,0:T(8,128)(2,1)S(1)}, f32[120,1,8,128]{3,2,1,0:T(8,128)S(1)}, f32[64,128]{1,0:T(8,128)S(1)}) custom-call(s32[1,128]{1,0:T(1,128)S(1)} %copy-done.6, s32[1,1024]{1,0:T(1,128)S(1)} %copy-done.5, bf16[512,128]{1,0:T(8,128)(2,1)S(1)} %copy-done.3, bf16[1024,256]{1,0:T(8,128)(2,1)S(1)} %bitcast.7, ...), custom_call_target="tpu_custom_call" | custom-call | tf_op jit(solution)/shard_map/section/pallas_call | solution.py:447
  80.3 2.0 %ending.1 = (bf16[1024,256]{1,0:T(8,128)(2,1)}, f32[512,128]{1,0:T(8,128)}, f32[27,64,64]{2,1,0:T(8,128)}, f32[64,128]{1,0:T(8,128)}) custom-call(s32[1,128]{1,0:T(1,128)S(1)} %copy-done.6, bf16[1024,128]{1,0:T(8,128)(2,1)S(1)} %get-tuple-element.12.back_ref, f32[120,1,8,128]{3,2,1,0:T(8,128)S(1)} %get-tuple-element.13.sums_ref, ...), custom_call_target="tpu_custom_call" | custom-call | tf_op jit(solution)/shard_map/ending/pallas_call | solution.py:512
Async XLA Ops:
  0.6 0.7 copy-start.5
  0.6 0.7 copy-start.6
  1.3 1.0 %copy-start = (bf16[64,1,16,256]{3,2,1,0:T(8,128)(2,1)S(1)}, bf16[64,1,16,256]{3,2,1,0:T(8,128)(2,1)}, u32[]{:S(2)}) copy-start(bf16[64,1,16,256]{3,2,1,0:T(8,128)(2,1)} %param.10) | copy-start | bytes 1572868
  2.4 1.0 %copy-start.1 = (bf16[64,1,16,256]{3,2,1,0:T(8,128)(2,1)S(1)}, bf16[64,1,16,256]{3,2,1,0:T(8,128)(2,1)}, u32[]{:S(2)}) copy-start(bf16[64,1,16,256]{3,2,1,0:T(8,128)(2,1)} %param.13) | copy-start | bytes 1572868
  3.4 1.0 %copy-start.2 = (bf16[27,64,64]{2,1,0:T(8,128)(2,1)S(1)}, bf16[27,64,64]{2,1,0:T(8,128)(2,1)}, u32[]{:S(2)}) copy-start(bf16[27,64,64]{2,1,0:T(8,128)(2,1)} %taps_ref.1) | copy-start | bytes 663556
  4.4 0.9 %copy-start.3 = (bf16[512,128]{1,0:T(8,128)(2,1)S(1)}, bf16[512,128]{1,0:T(8,128)(2,1)}, u32[]{:S(2)}) copy-start(bf16[512,128]{1,0:T(8,128)(2,1)} %rows_ref.1) | copy-start | bytes 393220
  5.3 0.7 copy-start.4

commit v2 on v1

--- a/solution.py
+++ b/solution.py
@@ -31,14 +31,18 @@
     counts_ref,
     cells_ref,
     rows_ref,
-    base_ref,
-    cot_ref,
-    taps_ref,
+    base_hbm,
+    cot_hbm,
+    taps_hbm,
     wpt_ref,
     out_ref,
     back_ref,
     sums_ref,
     psum_ref,
+    base_ref,
+    cot_ref,
+    taps_ref,
+    load_sem,
     send,
     arr,
     paint_a,
@@ -58,6 +62,7 @@
     near_in,
     acc,
     tiles,
+    pair_in,
     rs,
     ag,
     ptiles,
@@ -69,6 +74,7 @@
     rev_sem,
     cell_sem,
     near_sem,
+    pair_sem,
     rs_sem,
     ag_sem,
     prs_sem,
@@ -85,8 +91,8 @@
     cy, chans, nz = base.shape
     nslots = cells_ref.shape[1]
     cap = nslots // n
-    per = tiles.shape[1]
-    nconv = 120 // per
+    per = tiles.shape[2]
+    half = n // 2
     gi = lax.axis_index("gx")
     gj = lax.axis_index("gy")
     me = gi * ngy + gj
@@ -105,6 +111,15 @@
     @pl.loop(1, n)
     def _(k):
         pl.semaphore_signal(barrier, inc=1, device_id=coords(peer_of(k)), device_id_type=MESH)
+
+    loads = [
+        pltpu.make_async_copy(src, dst, load_sem.at[j])
+        for j, (src, dst) in enumerate(
+            ((base_hbm, base_ref), (taps_hbm, taps_ref), (cot_hbm, cot_ref))
+        )
+    ]
+    for load in loads:
+        load.start()
 
     counts = counts_ref[...].astype(F32)
     lane = lax.broadcasted_iota(jnp.int32, (nslots, n), 1)
@@ -166,6 +181,8 @@
     row = lax.broadcasted_iota(jnp.int32, (full, 1), 0)
     col = lax.broadcasted_iota(jnp.int32, (full, full), 1)
     perm[...] = (col == (row % chans) * cy + row // chans).astype(F32).astype(BF16)
+    for load in loads:
+        load.wait()
     base[...] = (
         jnp.dot(perm[...], base_ref[...], preferred_element_type=F32).astype(BF16).reshape(base.shape)
     )
@@ -228,9 +245,8 @@
         if first + count == cy:
             for copy in f_edges[0]:
                 copy.start()
-        if c < 2:
-            for copy in f_planes[c]:
-                copy.start()
+        for copy in f_planes[c]:
+            copy.start()
 
     for copy in cell_copies:
         copy.wait()
@@ -240,10 +256,7 @@
 
     for c, (first, count) in enumerate(F_ROWS):
         for copy in f_planes[c]:
-            copy.wait()
-        if c + 2 < len(F_CHUNKS):
-            for copy in f_planes[c + 2]:
-                copy.start()
+            copy.wait_recv()
         if c < 2:
             for copy in f_edges[c]:
                 copy.wait_recv()
@@ -267,9 +280,20 @@
         )
 
     per_row = acc.shape[1] // 128
-    for t in range(120):
+    for t in range(128):
         r, q = divmod(t, per_row)
-        tiles[t // per, t % per] = acc[8 * r : 8 * r + 8, 128 * q : 128 * q + 128]
+        share = t // per
+        if t < 120:
+            part = acc[8 * r : 8 * r + 8, 128 * q : 128 * q + 128]
+        else:
+            part = jnp.zeros((8, 128), F32)
+        tiles[share % 2, share // 2, t % per] = part
+    core = lax.rem(me, 2)
+    chip = lax.div(me, 2)
+    pair_copy = remote(
+        tiles.at[1 - core], pair_in, pair_sem.at[0], pair_sem.at[1], coords(me + 1 - 2 * core)
+    )
+    pair_copy.start()
 
     def scatter(src, dst, sems, count, step):
         @pl.loop(1, n)
@@ -316,7 +340,6 @@
             waits(dst, dst, sems, count).wait_send()
             waits(dst, dst, gather_sems, count).wait_recv()
 
-    scatter(tiles, rs, rs_sem, nconv, 1)
 
     for c, (first, count) in enumerate(((1, cy - 2), (0, 1), (cy - 1, 1))):
         if c == 1:
@@ -355,8 +378,16 @@
         )
         copy.start()
         near_copies.append(copy)
+    pair_copy.wait()
+    tiles[pl.ds(core, 1)] = tiles[pl.ds(core, 1)] + pair_in[...][None]
+
+    @pl.loop(1, half)
+    def _(k):
+        there = lax.rem(chip + k, half)
+        device = coords(2 * there + core)
+        remote(tiles.at[core, there], rs.at[chip], rs_sem.at[0], rs_sem.at[1], device).start()
+
     slot_grad = at_slots(1, 0, cell_y, at_slots(3, 0, cell_y, zero))
-    reduce_gather(tiles, rs, ag, rs_sem, ag_sem, nconv, 1)
     for copy in near_copies:
         copy.wait()
     slot_grad = slot_grad + near_in[0].astype(F32) + near_in[1].astype(F32)
@@ -371,6 +402,15 @@
     pcount = ptiles.shape[0]
     scatter(ptiles, prs, prs_sem, pcount, step)
 
+    waits(rs, rs, rs_sem, half - 1).wait_recv()
+    rs[pl.ds(chip, 1)] = tiles[core, pl.ds(chip, 1)]
+    ag[pl.ds(me, 1)] = jnp.sum(rs[...], axis=0, keepdims=True)
+
+    @pl.loop(1, n)
+    def _(k):
+        there = ag.at[me]
+        remote(there, there, ag_sem.at[0], ag_sem.at[1], coords(peer_of(k))).start()
+
     row = lax.broadcasted_iota(jnp.int32, (full, 1), 0)
     perm_back[...] = (col == (row % cy) * chans + row // cy).astype(F32).astype(BF16)
     out_ref[...] = jnp.dot(
@@ -380,14 +420,16 @@
     reduce_gather(ptiles, prs, pag, prs_sem, pag_sem, pcount, step)
     waits(sgs, sgr, rev_sem, n - 1).wait_recv()
     back_ref[...] = sgr[...].reshape(nslots, feats)
-    finish(rs, ag, rs_sem, ag_sem, nconv, 1)
-    sums_ref[...] = ag[:nconv]
+    waits(ag, ag, ag_sem, n - 1).wait_recv()
+    sums_ref[...] = ag[: sums_ref.shape[0]]
     finish(prs, pag, prs_sem, pag_sem, pcount, step)
     psum_ref[...] = pag[...].reshape(psum_ref.shape)
 
     waits(send, arr, a2a_sem, n - 1).wait_send()
     waits(sgs, sgr, rev_sem, n - 1).wait_send()
-    for copies in f_edges:
+    waits(rs, rs, rs_sem, half - 1).wait_send()
+    waits(ag, ag, ag_sem, n - 1).wait_send()
+    for copies in f_edges + f_planes:
         for copy in copies:
             copy.wait_send()
     for copy in g_edges:
@@ -452,9 +494,13 @@
             jax.ShapeDtypeStruct((120 // per, per, 8, 128), F32),
             jax.ShapeDtypeStruct((chans, feats), F32),
         ),
-        in_specs=[vmem] * 7,
+        in_specs=[vmem] * 3 + [pl.BlockSpec(memory_space=pl.ANY)] * 3 + [vmem],
         out_specs=[vmem] * 4,
         scratch_shapes=[
+            pltpu.VMEM((full, nz), BF16),
+            pltpu.VMEM((full, nz), BF16),
+            pltpu.VMEM((27, chans, chans), BF16),
+            dma((3,)),
             pltpu.VMEM((n, cap, feats), BF16),
             pltpu.VMEM((n, cap, feats), BF16),
             pltpu.VMEM((cy, chans, nslots), BF16),
@@ -473,8 +519,9 @@
             pltpu.VMEM((2, chans, nslots), BF16),
             pltpu.VMEM((2, chans, nslots), BF16),
             pltpu.VMEM((3 * chans, 640), F32),
-            pltpu.VMEM((n, per, 8, 128), F32),
-            pltpu.VMEM((n, per, 8, 128), F32),
+            pltpu.VMEM((2, n // 2, per, 8, 128), F32),
+            pltpu.VMEM((n // 2, per, 8, 128), F32),
+            pltpu.VMEM((n // 2, per, 8, 128), F32),
             pltpu.VMEM((n, per, 8, 128), F32),
             pltpu.VMEM((pcount, prow, feats), F32),
             pltpu.VMEM((n, prow, feats), F32),
@@ -489,6 +536,7 @@
             dma((2,)),
             dma((2,)),
             dma((2,)),
+            dma((2,)),
             dma((4, 2)),
             dma((4, 2)),
             dma((2, 3)),
@@ -497,7 +545,7 @@
             dma((2,)),
         ],
         compiler_params=pltpu.CompilerParams(
-            collective_id=0, has_side_effects=True, vmem_limit_bytes=44 * 1024 * 1024
+            collective_id=0, has_side_effects=True, vmem_limit_bytes=60 * 1024 * 1024
         ),
         name="section",
     )(
@@ -519,7 +567,7 @@
         ),
         in_specs=[vmem] * 6,
         out_specs=[vmem] * 4,
-        compiler_params=pltpu.CompilerParams(vmem_limit_bytes=16 * 1024 * 1024),
+        compiler_params=pltpu.CompilerParams(vmem_limit_bytes=60 * 1024 * 1024),
         name="ending",
     )(send_counts, back, sums, psum, out, weight_t)
     return out_field.reshape(base_field.shape), row_grads, conv_grad, proj_t.T

time: 82.7 us -> 74.6 us (0.902)
  local copies, waits for them, and re-layouts: 5.39 us -> 0 us
  Pallas kernels: 76.3 us -> 73.8 us
    unnamed x14 -> x0, local copies, waits for them, and re-layouts: 5.39 us -> none
    pallas_call x1, Pallas kernels: 74.3 us -> 70.5 us  [local(): pl.pallas_call(functools.partial(kernel, ngx, ngy), out_shape=(jax.ShapeD...]
    pallas_call x1, Pallas kernels: 2.01 us -> 3.32 us  [local(): pl.pallas_call(functools.partial(ending, cy * nz * n), out_shape=(jax.Sha...]
where the time goes in v2:
time: 74.6 us; the launch traced here: 74.4 us
  Pallas kernels  73.8 us (99%)
    pallas_call x1, Pallas kernels, local(): pl.pallas_call(functools.partial(kernel, ngx, ngy), out_shape=(jax.ShapeD...  70.5 us
    pallas_call x1, Pallas kernels, local(): pl.pallas_call(functools.partial(ending, cy * nz * n), out_shape=(jax.Sha...  3.32 us

profile of v2, /device:TPU:1, one launch (start us, length us, event | category | flops | bytes accessed | tf_op | source)
XLA Modules:
  0.0 74.4 jit_solution(18437774395055357987)
XLA Ops:
  0.6 70.5 %section.1 = (bf16[1024,256]{1,0:T(8,128)(2,1)}, bf16[1024,128]{1,0:T(8,128)(2,1)}, f32[120,1,8,128]{3,2,1,0:T(8,128)}, f32[64,128]{1,0:T(8,128)}) custom-call(s32[1,128]{1,0:T(1,128)} %counts_ref.3, s32[1,1024]{1,0:T(1,128)} %cells_ref.1, bf16[512,128]{1,0:T(8,128)(2,1)} %rows_ref.1, bf16[1024,256]{1,0:T(8,128)(2,1)} %bitcast.7, bf16[1024,256]{1,0:T(8,128)(2,1)} %bitcast.8, ...), custom_call_target="tpu_custom_call" | custom-call | tf_op jit(solution)/shard_map/section/pallas_call | solution.py:489
  71.1 3.3 %ending.1 = (bf16[1024,256]{1,0:T(8,128)(2,1)}, f32[512,128]{1,0:T(8,128)}, f32[27,64,64]{2,1,0:T(8,128)}, f32[64,128]{1,0:T(8,128)}) custom-call(s32[1,128]{1,0:T(1,128)} %counts_ref.3, bf16[1024,128]{1,0:T(8,128)(2,1)} %get-tuple-element.12.back_ref, f32[120,1,8,128]{3,2,1,0:T(8,128)} %get-tuple-element.13.sums_ref, f32[64,128]{1,0:T(8,128)} %get-tuple-element.14.psum_ref, ...), custom_call_target="tpu_custom_call" | custom-call | tf_op jit(solution)/shard_map/ending/pallas_call | solution.py:560

commit v3 on v2

--- a/solution.py
+++ b/solution.py
@@ -9,6 +9,7 @@
 from jax.sharding import PartitionSpec as P
 
 MESH = pl.DeviceIdType.MESH
+FLAT = pl.DeviceIdType.LOGICAL
 F32 = jnp.float32
 BF16 = jnp.bfloat16
 
@@ -67,7 +68,6 @@
     ag,
     ptiles,
     prs,
-    pag,
     sgs,
     sgr,
     a2a_sem,
@@ -78,7 +78,6 @@
     rs_sem,
     ag_sem,
     prs_sem,
-    pag_sem,
     fx_send,
     fx_recv,
     fy_send,
@@ -97,20 +96,44 @@
     gj = lax.axis_index("gy")
     me = gi * ngy + gj
 
-    def coords(d):
-        return (lax.div(d, ngy), lax.rem(d, ngy))
-
-    def peer_of(k):
-        return lax.rem(me + k, n)
+    low = 2 if ngx >= 8 else 1
+    dims = (ngx // (4 * low), 4, ngy // 2 * low, 2)
+    core = gj % 2
+    chip = me // 2
+    at = (gi // (4 * low), gi % 4, gj // 2 * low + gi // 4 % low, core)
+    moved = [[(at[a] + d) % dims[a] for d in range(dims[a])] for a in range(4)]
+    places = [
+        [v * (4 * low * ngy) for v in moved[0]],
+        [v * ngy for v in moved[1]],
+        [v % low * (4 * ngy) + v // low * 2 for v in moved[2]],
+        moved[3],
+    ]
+    steps = [
+        (a, b, c, d)
+        for a in range(dims[0])
+        for b in range(dims[1])
+        for c in range(dims[2])
+        for d in range(dims[3])
+        if (a, b, c, d) != (0, 0, 0, 0)
+    ]
+
+    def hops(step):
+        return -sum(min(v, size - v) for v, size in zip(step[:3], dims)), -step[3]
+
+    steps.sort(key=hops)
+    chips = [
+        [places[0][a] + places[1][b] for b in range(dims[1])] for a in range(dims[0])
+    ]
+    ends = [[places[2][c] + places[3][d] for d in range(2)] for c in range(dims[2])]
+    peers = [(chips[a][b] + ends[c][d], d) for a, b, c, d in steps]
 
     def beside(b):
         return (lax.rem(gi + b + ngx, ngx), gj)
 
     barrier = pltpu.get_barrier_semaphore()
 
-    @pl.loop(1, n)
-    def _(k):
-        pl.semaphore_signal(barrier, inc=1, device_id=coords(peer_of(k)), device_id_type=MESH)
+    for peer, _ in peers:
+        pl.semaphore_signal(barrier, inc=1, device_id=peer, device_id_type=FLAT)
 
     loads = [
         pltpu.make_async_copy(src, dst, load_sem.at[j])
@@ -142,20 +165,17 @@
             send_sem=send_sem,
             recv_sem=recv_sem,
             device_id=device,
-            device_id_type=MESH,
+            device_id_type=MESH if isinstance(device, tuple) else FLAT,
         )
 
     def spread(src, dst, sems):
-        @pl.loop(1, n)
-        def _(k):
-            peer = peer_of(k)
-            remote(src.at[peer], dst.at[me], sems.at[0], sems.at[1], coords(peer)).start()
-
+        for peer, _ in peers:
+            remote(src.at[peer], dst.at[me], sems.at[0], sems.at[1], peer).start()
         dst[pl.ds(me, 1)] = src[pl.ds(me, 1)]
 
     def waits(src, dst, sems, count):
         part = pl.ds(0, count)
-        return remote(src.at[part], dst.at[part], sems.at[0], sems.at[1], coords(peer_of(1)))
+        return remote(src.at[part], dst.at[part], sems.at[0], sems.at[1], peers[0][0])
 
     spread(send, arr, a2a_sem)
     cell_copies = [
@@ -254,6 +274,25 @@
     for e in (0, 1):
         paint_b[1 + e] = at_depth(near_cells[e])
 
+    def backward_row(y):
+        slab = pgr[y : y + 3].reshape(3 * chans, nz)
+        part = jnp.dot(wb[...], slab, preferred_element_type=F32)
+        for x in range(3):
+            p = part[3 * x * chans : 3 * (x + 1) * chans]
+            got = roll_z(p[:chans], 1) + p[chans : 2 * chans] + roll_z(p[2 * chans :], -1)
+            if x == 1:
+                got = got + cot[y].astype(F32)
+                high = got.astype(BF16)
+                grads[3, y] = (got - high.astype(F32)).astype(BF16)
+                grads[1, y] = high
+            else:
+                grads[x, y] = got.astype(BF16)
+
+    def tap_terms(slabs, threes):
+        acc[:, : N_TAPS * chans] += nt_dot(
+            jnp.concatenate(threes, axis=1), jnp.concatenate(slabs, axis=1)
+        )
+
     for c, (first, count) in enumerate(F_ROWS):
         for copy in f_planes[c]:
             copy.wait_recv()
@@ -275,89 +314,18 @@
             threes.append(three.astype(BF16))
         if c < 2:
             g_edges[1 - c].start()
-        acc[:, : N_TAPS * chans] += nt_dot(
-            jnp.concatenate(threes, axis=1), jnp.concatenate(slabs, axis=1)
-        )
-
-    per_row = acc.shape[1] // 128
-    for t in range(128):
-        r, q = divmod(t, per_row)
-        share = t // per
-        if t < 120:
-            part = acc[8 * r : 8 * r + 8, 128 * q : 128 * q + 128]
-        else:
-            part = jnp.zeros((8, 128), F32)
-        tiles[share % 2, share // 2, t % per] = part
-    core = lax.rem(me, 2)
-    chip = lax.div(me, 2)
-    pair_copy = remote(
-        tiles.at[1 - core], pair_in, pair_sem.at[0], pair_sem.at[1], coords(me + 1 - 2 * core)
-    )
-    pair_copy.start()
-
-    def scatter(src, dst, sems, count, step):
-        @pl.loop(1, n)
-        def _(k):
-            peer = peer_of(k)
-            share = lax.div(peer, step)
-
-            @pl.when((share < count) & (share * step == peer))
-            def _():
-                remote(src.at[share], dst.at[me], sems.at[0], sems.at[1], coords(peer)).start()
-
-    def mine_of(count, step):
-        share = lax.div(me, step)
-        return share, (share < count) & (share * step == me)
-
-    def reduce_gather(src, part, dst, sems, gather_sems, count, step):
-        share, own = mine_of(count, step)
-
-        @pl.when(own)
-        def _():
-            waits(part, part, sems, n - 1).wait_recv()
-            part[pl.ds(me, 1)] = src[pl.ds(share, 1)]
-            dst[pl.ds(share, 1)] = jnp.sum(part[...], axis=0, keepdims=True)
-
-            @pl.loop(1, n)
-            def _(k):
-                there = dst.at[share]
-                remote(
-                    there, there, gather_sems.at[0], gather_sems.at[1], coords(peer_of(k))
-                ).start()
-
-    def finish(part, dst, sems, gather_sems, count, step):
-        _, own = mine_of(count, step)
-
-        @pl.when(own)
-        def _():
-            waits(part, part, gather_sems, n - 1).wait_send()
-            if count > 1:
-                waits(dst, dst, sems, count - 1).wait_send()
-                waits(dst, dst, gather_sems, count - 1).wait_recv()
-
-        @pl.when(jnp.logical_not(own))
-        def _():
-            waits(dst, dst, sems, count).wait_send()
-            waits(dst, dst, gather_sems, count).wait_recv()
-
-
-    for c, (first, count) in enumerate(((1, cy - 2), (0, 1), (cy - 1, 1))):
-        if c == 1:
-            for copy in g_edges:
-                copy.wait_recv()
-        for y in range(first, first + count):
-            slab = pgr[y : y + 3].reshape(3 * chans, nz)
-            part = jnp.dot(wb[...], slab, preferred_element_type=F32)
-            for x in range(3):
-                p = part[3 * x * chans : 3 * (x + 1) * chans]
-                got = roll_z(p[:chans], 1) + p[chans : 2 * chans] + roll_z(p[2 * chans :], -1)
-                if x == 1:
-                    got = got + cot[y].astype(F32)
-                    high = got.astype(BF16)
-                    grads[3, y] = (got - high.astype(F32)).astype(BF16)
-                    grads[1, y] = high
-                else:
-                    grads[x, y] = got.astype(BF16)
+        if c < 3:
+            tap_terms(slabs, threes)
+        if c == 2:
+            for y in (1, 2, 3, 4, 5, 14):
+                backward_row(y)
+
+    for y in range(6, 14):
+        backward_row(y)
+    for copy in g_edges:
+        copy.wait_recv()
+    backward_row(0)
+    backward_row(15)
 
     def at_slots(which, depth, ys, total):
         step = 4
@@ -378,16 +346,32 @@
         )
         copy.start()
         near_copies.append(copy)
+
+    tap_terms(slabs, threes)
+    per_row = acc.shape[1] // 128
+    proj_shares = 8 // per
+    stride = n // proj_shares
+    proj_at = [stride * m + 5 * (m % 4) for m in range(proj_shares)]
+    conv_at = [d for d in range(n) if d not in proj_at]
+    for t in range(120):
+        r, q = divmod(t, per_row)
+        d = conv_at[t // per]
+        tiles[d % 2, d // 2, t % per] = acc[8 * r : 8 * r + 8, 128 * q : 128 * q + 128]
+    for d in proj_at:
+        tiles[d % 2, d // 2] = jnp.zeros((per, 8, 128), F32)
+    pair_copy = remote(
+        tiles.at[1 - core], pair_in, pair_sem.at[0], pair_sem.at[1], me + 1 - 2 * core
+    )
+    pair_copy.start()
+    slot_grad = at_slots(1, 0, cell_y, at_slots(3, 0, cell_y, zero))
     pair_copy.wait()
     tiles[pl.ds(core, 1)] = tiles[pl.ds(core, 1)] + pair_in[...][None]
-
-    @pl.loop(1, half)
-    def _(k):
-        there = lax.rem(chip + k, half)
-        device = coords(2 * there + core)
-        remote(tiles.at[core, there], rs.at[chip], rs_sem.at[0], rs_sem.at[1], device).start()
-
-    slot_grad = at_slots(1, 0, cell_y, at_slots(3, 0, cell_y, zero))
+    for peer, d in peers:
+        if d == 0:
+            remote(
+                tiles.at[core, peer // 2], rs.at[chip], rs_sem.at[0], rs_sem.at[1], peer
+            ).start()
+
     for copy in near_copies:
         copy.wait()
     slot_grad = slot_grad + near_in[0].astype(F32) + near_in[1].astype(F32)
@@ -397,19 +381,35 @@
     sgs[...] = wide.T.astype(BF16).reshape(sgs.shape)
     spread(sgs, sgr, rev_sem)
     proj_part = jnp.dot(slot_grad, arrived, preferred_element_type=F32)
-    ptiles[...] = proj_part.reshape(ptiles.shape)
-    step = n // min(n, chans)
-    pcount = ptiles.shape[0]
-    scatter(ptiles, prs, prs_sem, pcount, step)
+    for t in range(8):
+        ptiles[t // per, t % per] = proj_part[8 * t : 8 * t + 8]
+    group = me // stride
+    proj_owner = me % stride == 5 * (group % 4)
+    for m, d in enumerate(proj_at):
+
+        @pl.when(me != d)
+        def _(m=m, d=d):
+            remote(ptiles.at[m], prs.at[me], prs_sem.at[0], prs_sem.at[1], d).start()
+
+    def gather():
+        there = ag.at[me]
+        for peer, _ in peers:
+            remote(there, there, ag_sem.at[0], ag_sem.at[1], peer).start()
 
     waits(rs, rs, rs_sem, half - 1).wait_recv()
-    rs[pl.ds(chip, 1)] = tiles[core, pl.ds(chip, 1)]
-    ag[pl.ds(me, 1)] = jnp.sum(rs[...], axis=0, keepdims=True)
-
-    @pl.loop(1, n)
-    def _(k):
-        there = ag.at[me]
-        remote(there, there, ag_sem.at[0], ag_sem.at[1], coords(peer_of(k))).start()
+
+    @pl.when(jnp.logical_not(proj_owner))
+    def _():
+        rs[pl.ds(chip, 1)] = tiles[core, pl.ds(chip, 1)]
+        ag[pl.ds(me, 1)] = jnp.sum(rs[...], axis=0, keepdims=True)
+        gather()
+
+    @pl.when(proj_owner)
+    def _():
+        waits(prs, prs, prs_sem, n - 1).wait_recv()
+        prs[pl.ds(me, 1)] = ptiles[pl.ds(group, 1)]
+        ag[pl.ds(me, 1)] = jnp.sum(prs[...], axis=0, keepdims=True)
+        gather()
 
     row = lax.broadcasted_iota(jnp.int32, (full, 1), 0)
     perm_back[...] = (col == (row % cy) * chans + row // cy).astype(F32).astype(BF16)
@@ -417,13 +417,22 @@
         perm_back[...], outs[...].reshape(full, nz), preferred_element_type=F32
     ).astype(BF16)
 
-    reduce_gather(ptiles, prs, pag, prs_sem, pag_sem, pcount, step)
     waits(sgs, sgr, rev_sem, n - 1).wait_recv()
     back_ref[...] = sgr[...].reshape(nslots, feats)
     waits(ag, ag, ag_sem, n - 1).wait_recv()
-    sums_ref[...] = ag[: sums_ref.shape[0]]
-    finish(prs, pag, prs_sem, pag_sem, pcount, step)
-    psum_ref[...] = pag[...].reshape(psum_ref.shape)
+    for t in range(120):
+        sums_ref[t // per, t % per] = ag[conv_at[t // per], t % per]
+    for t in range(8):
+        psum_ref[8 * t : 8 * t + 8] = ag[proj_at[t // per], t % per]
+
+    @pl.when(proj_owner)
+    def _():
+        if proj_shares > 1:
+            waits(ptiles, ptiles, prs_sem, proj_shares - 1).wait_send()
+
+    @pl.when(jnp.logical_not(proj_owner))
+    def _():
+        waits(ptiles, ptiles, prs_sem, proj_shares).wait_send()
 
     waits(send, arr, a2a_sem, n - 1).wait_send()
     waits(sgs, sgr, rev_sem, n - 1).wait_send()
@@ -480,8 +489,6 @@
     full = chans * cy
     cap = nslots // n
     per = 128 // n
-    pcount = min(n, chans)
-    prow = chans // pcount
     weight_t = proj_weight.T
     dma = pltpu.SemaphoreType.DMA
     vmem = pl.BlockSpec(memory_space=pltpu.VMEM)
@@ -523,16 +530,14 @@
             pltpu.VMEM((n // 2, per, 8, 128), F32),
             pltpu.VMEM((n // 2, per, 8, 128), F32),
             pltpu.VMEM((n, per, 8, 128), F32),
-            pltpu.VMEM((pcount, prow, feats), F32),
-            pltpu.VMEM((n, prow, feats), F32),
-            pltpu.VMEM((pcount, prow, feats), F32),
+            pltpu.VMEM((8 // per, per, 8, 128), F32),
+            pltpu.VMEM((n, per, 8, 128), F32),
             pltpu.VMEM((n, cap, feats), BF16),
             pltpu.VMEM((n, cap, feats), BF16),
             dma((2,)),
             dma((2,)),
             dma((2, 2)),
             dma((2, 2)),
-            dma((2,)),
             dma((2,)),
             dma((2,)),
             dma((2,)),

time: 74.6 us -> 70.8 us (0.949)
  Pallas kernels: 73.8 us -> 70.1 us
    pallas_call x1, Pallas kernels: 70.5 us -> 66.7 us  [local(): pl.pallas_call(functools.partial(kernel, ngx, ngy), out_shape=(jax.ShapeD...]
where the time goes in v3:
time: 70.8 us; the launch traced here: 70.7 us
  Pallas kernels  70.1 us (99%)
    pallas_call x1, Pallas kernels, local(): pl.pallas_call(functools.partial(kernel, ngx, ngy), out_shape=(jax.ShapeD...  66.7 us
    pallas_call x1, Pallas kernels, local(): pl.pallas_call(functools.partial(ending, cy * nz * n), out_shape=(jax.Sha...  3.32 us

profile of v3, /device:TPU:1, one launch (start us, length us, event | category | flops | bytes accessed | tf_op | source)
XLA Modules:
  0.0 70.7 jit_solution(18137403580982799722)
XLA Ops:
  0.6 66.7 %section.1 = (bf16[1024,256]{1,0:T(8,128)(2,1)}, bf16[1024,128]{1,0:T(8,128)(2,1)}, f32[120,1,8,128]{3,2,1,0:T(8,128)}, f32[64,128]{1,0:T(8,128)}) custom-call(s32[1,128]{1,0:T(1,128)} %counts_ref.3, s32[1,1024]{1,0:T(1,128)} %cells_ref.1, bf16[512,128]{1,0:T(8,128)(2,1)} %rows_ref.1, bf16[1024,256]{1,0:T(8,128)(2,1)} %bitcast.7, bf16[1024,256]{1,0:T(8,128)(2,1)} %bitcast.8, ...), custom_call_target="tpu_custom_call" | custom-call | tf_op jit(solution)/shard_map/section/pallas_call | solution.py:496
  67.4 3.3 %ending.1 = (bf16[1024,256]{1,0:T(8,128)(2,1)}, f32[512,128]{1,0:T(8,128)}, f32[27,64,64]{2,1,0:T(8,128)}, f32[64,128]{1,0:T(8,128)}) custom-call(s32[1,128]{1,0:T(1,128)} %counts_ref.3, bf16[1024,128]{1,0:T(8,128)(2,1)} %get-tuple-element.12.back_ref, f32[120,1,8,128]{3,2,1,0:T(8,128)} %get-tuple-element.13.sums_ref, f32[64,128]{1,0:T(8,128)} %get-tuple-element.14.psum_ref, ...), custom_call_target="tpu_custom_call" | custom-call | tf_op jit(solution)/shard_map/ending/pallas_call | solution.py:565

commit v4 on v3

--- a/solution.py
+++ b/solution.py
@@ -13,8 +13,11 @@
 F32 = jnp.float32
 BF16 = jnp.bfloat16
 
-F_CHUNKS = ((0, 4), (12, 4), (4, 4), (8, 4))
-F_ROWS = ((0, 3), (13, 3), (3, 4), (7, 6))
+F_CHUNKS = ((0, 4), (12, 4), (4, 3), (7, 3), (10, 2))
+F_ROWS = ((0, 3), (13, 3), (3, 3), (6, 3), (9, 4))
+G_ROWS = ((), (), (1, 2, 3, 4, 14), (5, 6, 7, 0, 15), (8, 9, 10, 11, 12, 13))
+EARLY = ((0, 4), (4, 4), (14, 2))
+LATE = ((8, 3), (11, 3))
 N_TAPS = 9
 
 
@@ -37,7 +40,7 @@
     taps_hbm,
     wpt_ref,
     out_ref,
-    back_ref,
+    rowg_ref,
     sums_ref,
     psum_ref,
     base_ref,
@@ -46,6 +49,7 @@
     load_sem,
     send,
     arr,
+    onehot_t,
     paint_a,
     paint_b,
     perm,
@@ -68,6 +72,7 @@
     ag,
     ptiles,
     prs,
+    pag,
     sgs,
     sgr,
     a2a_sem,
@@ -78,6 +83,8 @@
     rs_sem,
     ag_sem,
     prs_sem,
+    pag_sem,
+    share_sem,
     fx_send,
     fx_recv,
     fy_send,
@@ -219,14 +226,25 @@
                 side = (2 - y) * chans
                 wb[at : at + chans, side : side + chans] = tap.astype(F32).T.astype(BF16)
     acc[...] = jnp.zeros_like(acc)
+    upper = lax.broadcasted_iota(jnp.int32, (n, n), 0) <= lax.broadcasted_iota(jnp.int32, (n, n), 1)
+    ends_at = jnp.dot(
+        jnp.broadcast_to(counts, (8, n)).astype(BF16),
+        upper.astype(F32).astype(BF16),
+        preferred_element_type=F32,
+    )[:1]
+    order = lax.broadcasted_iota(jnp.int32, (nrows, 1), 0)
+    below = ends_at <= order.astype(F32)
+    owner_of = jnp.sum(jnp.where(below, 1.0, 0.0), axis=1, keepdims=True)
+    start_of = jnp.max(jnp.where(below, ends_at, 0.0), axis=1, keepdims=True)
+    slot_of = (owner_of * cap - start_of).astype(jnp.int32) + order
+    hit = lax.broadcasted_iota(jnp.int32, (nrows, nslots), 1) == slot_of
+    onehot_t[...] = hit.astype(F32).astype(BF16)
+    perm_back[...] = (col == (row % cy) * chans + row // cy).astype(F32).astype(BF16)
 
     waits(send, arr, a2a_sem, n - 1).wait_recv()
 
     arrived = arr[...].reshape(nslots, feats)
     projected = nt_dot(wpt_ref[...], arrived).astype(BF16).astype(F32)
-    for y in range(cy):
-        paint_a[y] = jnp.where(cell_y == y, projected, 0.0).astype(BF16)
-
     def edge_copy(side, b):
         to = (lax.rem(gi + b + ngx, ngx), lax.rem(gj + (1 if side == 0 else ngy - 1), ngy))
         row = cy if side == 0 else 1
@@ -256,6 +274,8 @@
 
     for c, (first, count) in enumerate(F_CHUNKS):
         rows = slice(first, first + count)
+        for y in range(first, first + count):
+            paint_a[y] = jnp.where(cell_y == y, projected, 0.0).astype(BF16)
         painted = nt_dot(paint_a[rows].reshape(count * chans, nslots), paint_b[0])
         painted = painted.reshape(count, chans, nz)
         fld[first + 1 : first + count + 1, 1] = (base[rows].astype(F32) + painted).astype(BF16)
@@ -293,6 +313,17 @@
             jnp.concatenate(threes, axis=1), jnp.concatenate(slabs, axis=1)
         )
 
+    def at_slots(which, depth, ys, total, ranges):
+        for first, count in ranges:
+            rows = grads[which, first : first + count].reshape(count * chans, nz)
+            got = jnp.dot(rows, paint_b[depth], preferred_element_type=F32)
+            for y in range(count):
+                part = got[y * chans : (y + 1) * chans]
+                total = total + jnp.where(ys == first + y, part, 0.0)
+        return total
+
+    zero = jnp.zeros((chans, nslots), F32)
+    late_slabs, late_threes = [], []
     for c, (first, count) in enumerate(F_ROWS):
         for copy in f_planes[c]:
             copy.wait_recv()
@@ -316,38 +347,27 @@
             g_edges[1 - c].start()
         if c < 3:
             tap_terms(slabs, threes)
-        if c == 2:
-            for y in (1, 2, 3, 4, 5, 14):
-                backward_row(y)
-
-    for y in range(6, 14):
-        backward_row(y)
-    for copy in g_edges:
-        copy.wait_recv()
-    backward_row(0)
-    backward_row(15)
-
-    def at_slots(which, depth, ys, total):
-        step = 4
-        for first in range(0, cy, step):
-            rows = grads[which, first : first + step].reshape(step * chans, nz)
-            got = jnp.dot(rows, paint_b[depth], preferred_element_type=F32)
-            for y in range(step):
-                part = got[y * chans : (y + 1) * chans]
-                total = total + jnp.where(ys == first + y, part, 0.0)
-        return total
-
-    zero = jnp.zeros((chans, nslots), F32)
+        else:
+            late_slabs += slabs
+            late_threes += threes
+        if c == 3:
+            for copy in g_edges:
+                copy.wait_recv()
+        for y in G_ROWS[c]:
+            backward_row(y)
+        if c == 3:
+            sums = [at_slots(2 * e, 1 + e, near_y[e], zero, EARLY) for e in (0, 1)]
+
     near_copies = []
     for e, b in ((0, -1), (1, 1)):
-        near_out[e] = at_slots(1 + b, 1 + e, near_y[e], zero).astype(BF16)
+        near_out[e] = at_slots(2 * e, 1 + e, near_y[e], sums[e], LATE).astype(BF16)
         copy = remote(
             near_out.at[e], near_in.at[1 - e], near_sem.at[0, e], near_sem.at[1, 1 - e], beside(b)
         )
         copy.start()
         near_copies.append(copy)
 
-    tap_terms(slabs, threes)
+    tap_terms(late_slabs, late_threes)
     per_row = acc.shape[1] // 128
     proj_shares = 8 // per
     stride = n // proj_shares
@@ -363,7 +383,8 @@
         tiles.at[1 - core], pair_in, pair_sem.at[0], pair_sem.at[1], me + 1 - 2 * core
     )
     pair_copy.start()
-    slot_grad = at_slots(1, 0, cell_y, at_slots(3, 0, cell_y, zero))
+    slot_grad = at_slots(3, 0, cell_y, zero, EARLY + LATE)
+    slot_grad = at_slots(1, 0, cell_y, slot_grad, EARLY + LATE)
     pair_copy.wait()
     tiles[pl.ds(core, 1)] = tiles[pl.ds(core, 1)] + pair_in[...][None]
     for peer, d in peers:
@@ -371,6 +392,10 @@
             remote(
                 tiles.at[core, peer // 2], rs.at[chip], rs_sem.at[0], rs_sem.at[1], peer
             ).start()
+
+    out_ref[...] = jnp.dot(
+        perm_back[...], outs[...].reshape(full, nz), preferred_element_type=F32
+    ).astype(BF16)
 
     for copy in near_copies:
         copy.wait()
@@ -391,53 +416,59 @@
         def _(m=m, d=d):
             remote(ptiles.at[m], prs.at[me], prs_sem.at[0], prs_sem.at[1], d).start()
 
-    def gather():
-        there = ag.at[me]
-        for peer, _ in peers:
+    waits(rs, rs, rs_sem, half - 1).wait_recv()
+    rs[pl.ds(chip, 1)] = tiles[core, pl.ds(chip, 1)]
+    ag[core, pl.ds(chip, 1)] = jnp.sum(rs[...], axis=0, keepdims=True)
+    there = ag.at[core, chip]
+    for peer, d in peers:
+        if d == 0:
             remote(there, there, ag_sem.at[0], ag_sem.at[1], peer).start()
-
-    waits(rs, rs, rs_sem, half - 1).wait_recv()
-
-    @pl.when(jnp.logical_not(proj_owner))
-    def _():
-        rs[pl.ds(chip, 1)] = tiles[core, pl.ds(chip, 1)]
-        ag[pl.ds(me, 1)] = jnp.sum(rs[...], axis=0, keepdims=True)
-        gather()
 
     @pl.when(proj_owner)
     def _():
         waits(prs, prs, prs_sem, n - 1).wait_recv()
         prs[pl.ds(me, 1)] = ptiles[pl.ds(group, 1)]
-        ag[pl.ds(me, 1)] = jnp.sum(prs[...], axis=0, keepdims=True)
-        gather()
-
-    row = lax.broadcasted_iota(jnp.int32, (full, 1), 0)
-    perm_back[...] = (col == (row % cy) * chans + row // cy).astype(F32).astype(BF16)
-    out_ref[...] = jnp.dot(
-        perm_back[...], outs[...].reshape(full, nz), preferred_element_type=F32
-    ).astype(BF16)
-
+        pag[pl.ds(group, 1)] = jnp.sum(prs[...], axis=0, keepdims=True)
+        for peer, _ in peers:
+            remote(pag.at[group], pag.at[group], pag_sem.at[0], pag_sem.at[1], peer).start()
+
+    waits(rs, rs, ag_sem, half - 1).wait_recv()
+    share_copy = remote(
+        ag.at[core], ag.at[core], share_sem.at[0], share_sem.at[1], me + 1 - 2 * core
+    )
+    share_copy.start()
     waits(sgs, sgr, rev_sem, n - 1).wait_recv()
-    back_ref[...] = sgr[...].reshape(nslots, feats)
-    waits(ag, ag, ag_sem, n - 1).wait_recv()
+    back = sgr[...].reshape(nslots, feats)
+    back = jnp.dot(onehot_t[...], back, preferred_element_type=F32)
+    rowg_ref[...] = jnp.dot(
+        back[:, :chans].astype(BF16), wpt_ref[...], preferred_element_type=F32
+    )
+    remote(
+        ag.at[core], ag.at[1 - core], share_sem.at[0], share_sem.at[1], me + 1 - 2 * core
+    ).wait()
     for t in range(120):
-        sums_ref[t // per, t % per] = ag[conv_at[t // per], t % per]
-    for t in range(8):
-        psum_ref[8 * t : 8 * t + 8] = ag[proj_at[t // per], t % per]
+        d = conv_at[t // per]
+        sums_ref[t // per, t % per] = ag[d % 2, d // 2, t % per]
 
     @pl.when(proj_owner)
     def _():
+        waits(prs, prs, pag_sem, n - 1).wait_send()
         if proj_shares > 1:
             waits(ptiles, ptiles, prs_sem, proj_shares - 1).wait_send()
+            waits(ptiles, ptiles, pag_sem, proj_shares - 1).wait_recv()
 
     @pl.when(jnp.logical_not(proj_owner))
     def _():
         waits(ptiles, ptiles, prs_sem, proj_shares).wait_send()
+        waits(ptiles, ptiles, pag_sem, proj_shares).wait_recv()
+
+    for t in range(8):
+        psum_ref[8 * t : 8 * t + 8] = pag[t // per, t % per]
 
     waits(send, arr, a2a_sem, n - 1).wait_send()
     waits(sgs, sgr, rev_sem, n - 1).wait_send()
     waits(rs, rs, rs_sem, half - 1).wait_send()
-    waits(ag, ag, ag_sem, n - 1).wait_send()
+    waits(rs, rs, ag_sem, half - 1).wait_send()
     for copies in f_edges + f_planes:
         for copy in copies:
             copy.wait_send()
@@ -445,40 +476,22 @@
         copy.wait_send()
 
 
-def ending(
-    count_all, counts_ref, back_ref, sums_ref, psum_ref, outf_ref, wpt_ref, out_ref, rowg_ref, convg_ref, projg_ref
-):
-    n = counts_ref.shape[1]
-    nslots, feats = back_ref.shape
-    chans = wpt_ref.shape[0]
-    nrows = rowg_ref.shape[0]
-    cap = nslots // n
+def ending(conv_scale, proj_scale, rows_ref, sums_ref, psum_ref, outf_ref, out_ref, rowg_ref, convg_ref, projg_ref):
     out_ref[...] = outf_ref[...]
-    counts = jnp.broadcast_to(counts_ref[...].astype(F32), (8, n)).astype(BF16)
-    upper = lax.broadcasted_iota(jnp.int32, (n, n), 0) <= lax.broadcasted_iota(jnp.int32, (n, n), 1)
-    ends = jnp.dot(counts, upper.astype(F32).astype(BF16), preferred_element_type=F32)[:1]
-    places = lax.broadcasted_iota(jnp.int32, (nrows, 1), 0)
-    below = ends <= places.astype(F32)
-    owner_of = jnp.sum(jnp.where(below, 1.0, 0.0), axis=1, keepdims=True)
-    start_of = jnp.max(jnp.where(below, ends, 0.0), axis=1, keepdims=True)
-    slot_of = (owner_of * cap - start_of).astype(jnp.int32) + places
-    hit = lax.broadcasted_iota(jnp.int32, (nrows, nslots), 1) == slot_of
-    back = jnp.dot(hit.astype(F32).astype(BF16), back_ref[...], preferred_element_type=F32)
-    rowg_ref[...] = jnp.dot(
-        back[:, :chans].astype(BF16), wpt_ref[...], preferred_element_type=F32
-    )
+    rowg_ref[...] = rows_ref[...]
     per = sums_ref.shape[1]
+    chans = convg_ref.shape[1]
     rows = []
     for r in range(3 * chans // 8):
         tiles = [sums_ref[t // per, t % per] for t in range(5 * r, 5 * r + 5)]
         rows.append(jnp.concatenate(tiles, axis=1))
-    sums = jnp.concatenate(rows, axis=0) * (1.0 / math.sqrt(count_all))
+    sums = jnp.concatenate(rows, axis=0) * conv_scale
     for x in range(3):
         for y in range(3):
             for z in range(3):
                 at = (y * 3 + x) * chans
                 convg_ref[x * 9 + y * 3 + z] = sums[z * chans : (z + 1) * chans, at : at + chans]
-    projg_ref[...] = psum_ref[...] * (1.0 / math.sqrt(nrows * n))
+    projg_ref[...] = psum_ref[...] * proj_scale
 
 
 def local(ngx, ngy, particles, send_counts, cell_lists, base_field, proj_weight, conv_weight, cotangent):
@@ -493,11 +506,11 @@
     dma = pltpu.SemaphoreType.DMA
     vmem = pl.BlockSpec(memory_space=pltpu.VMEM)
     plane = (cy, chans, nz)
-    out, back, sums, psum = pl.pallas_call(
+    out, rows, sums, psum = pl.pallas_call(
         functools.partial(kernel, ngx, ngy),
         out_shape=(
             jax.ShapeDtypeStruct((full, nz), BF16),
-            jax.ShapeDtypeStruct((nslots, feats), BF16),
+            jax.ShapeDtypeStruct((nrows, feats), F32),
             jax.ShapeDtypeStruct((120 // per, per, 8, 128), F32),
             jax.ShapeDtypeStruct((chans, feats), F32),
         ),
@@ -510,6 +523,7 @@
             dma((3,)),
             pltpu.VMEM((n, cap, feats), BF16),
             pltpu.VMEM((n, cap, feats), BF16),
+            pltpu.VMEM((nrows, nslots), BF16),
             pltpu.VMEM((cy, chans, nslots), BF16),
             pltpu.VMEM((3, nz, nslots), BF16),
             pltpu.VMEM((full, full), BF16),
@@ -529,9 +543,10 @@
             pltpu.VMEM((2, n // 2, per, 8, 128), F32),
             pltpu.VMEM((n // 2, per, 8, 128), F32),
             pltpu.VMEM((n // 2, per, 8, 128), F32),
+            pltpu.VMEM((2, n // 2, per, 8, 128), F32),
+            pltpu.VMEM((8 // per, per, 8, 128), F32),
             pltpu.VMEM((n, per, 8, 128), F32),
             pltpu.VMEM((8 // per, per, 8, 128), F32),
-            pltpu.VMEM((n, per, 8, 128), F32),
             pltpu.VMEM((n, cap, feats), BF16),
             pltpu.VMEM((n, cap, feats), BF16),
             dma((2,)),
@@ -542,8 +557,10 @@
             dma((2,)),
             dma((2,)),
             dma((2,)),
-            dma((4, 2)),
-            dma((4, 2)),
+            dma((2,)),
+            dma((2,)),
+            dma((5, 2)),
+            dma((5, 2)),
             dma((2, 3)),
             dma((2, 3)),
             dma((2,)),
@@ -563,18 +580,18 @@
         weight_t,
     )
     out_field, row_grads, conv_grad, proj_t = pl.pallas_call(
-        functools.partial(ending, cy * nz * n),
+        functools.partial(ending, 1.0 / math.sqrt(cy * nz * n), 1.0 / math.sqrt(nrows * n)),
         out_shape=(
             jax.ShapeDtypeStruct((full, nz), BF16),
             jax.ShapeDtypeStruct((nrows, feats), F32),
             jax.ShapeDtypeStruct((27, chans, chans), F32),
             jax.ShapeDtypeStruct((chans, feats), F32),
         ),
-        in_specs=[vmem] * 6,
+        in_specs=[vmem] * 4,
         out_specs=[vmem] * 4,
         compiler_params=pltpu.CompilerParams(vmem_limit_bytes=60 * 1024 * 1024),
         name="ending",
-    )(send_counts, back, sums, psum, out, weight_t)
+    )(rows, sums, psum, out)
     return out_field.reshape(base_field.shape), row_grads, conv_grad, proj_t.T
 
 

time: 70.8 us -> 69.4 us (0.980)
  Pallas kernels: 70.1 us -> 68.6 us
    pallas_call x1, Pallas kernels: 3.32 us -> 2.58 us  [local(): pl.pallas_call(functools.partial(ending, 1.0 / math.sqrt(cy * nz * n), 1....]
where the time goes in v4:
time: 69.4 us; the launch traced here: 69.3 us
  Pallas kernels  68.6 us (99%)
    pallas_call x1, Pallas kernels, local(): pl.pallas_call(functools.partial(kernel, ngx, ngy), out_shape=(jax.ShapeD...  66.1 us
    pallas_call x1, Pallas kernels, local(): pl.pallas_call(functools.partial(ending, 1.0 / math.sqrt(cy * nz * n), 1....  2.58 us

profile of v4, /device:TPU:1, one launch (start us, length us, event | category | flops | bytes accessed | tf_op | source)
XLA Modules:
  0.0 69.3 jit_solution(4875650048207309433)
XLA Ops:
  0.6 66.1 %section.1 = (bf16[1024,256]{1,0:T(8,128)(2,1)}, f32[512,128]{1,0:T(8,128)}, f32[120,1,8,128]{3,2,1,0:T(8,128)}, f32[64,128]{1,0:T(8,128)}) custom-call(s32[1,128]{1,0:T(1,128)} %counts_ref.1, s32[1,1024]{1,0:T(1,128)} %cells_ref.1, bf16[512,128]{1,0:T(8,128)(2,1)} %rows_ref.1, bf16[1024,256]{1,0:T(8,128)(2,1)} %bitcast.7, bf16[1024,256]{1,0:T(8,128)(2,1)} %bitcast.8, ...), custom_call_target="tpu_custom_call" | custom-call | tf_op jit(solution)/shard_map/section/pallas_call | solution.py:509
  66.7 2.6 %ending.1 = (bf16[1024,256]{1,0:T(8,128)(2,1)}, f32[512,128]{1,0:T(8,128)}, f32[27,64,64]{2,1,0:T(8,128)}, f32[64,128]{1,0:T(8,128)}) custom-call(f32[512,128]{1,0:T(8,128)} %get-tuple-element.12.rows_ref, f32[120,1,8,128]{3,2,1,0:T(8,128)} %get-tuple-element.13.sums_ref, f32[64,128]{1,0:T(8,128)} %get-tuple-element.14.psum_ref, ...), custom_call_target="tpu_custom_call" | custom-call | tf_op jit(solution)/shard_map/ending/pallas_call | solution.py:582

commit v5 on v4

--- a/solution.py
+++ b/solution.py
@@ -345,7 +345,7 @@
             threes.append(three.astype(BF16))
         if c < 2:
             g_edges[1 - c].start()
-        if c < 3:
+        if c < 2:
             tap_terms(slabs, threes)
         else:
             late_slabs += slabs
@@ -402,9 +402,6 @@
     slot_grad = slot_grad + near_in[0].astype(F32) + near_in[1].astype(F32)
 
     slot_grad = slot_grad.astype(BF16)
-    wide = jnp.concatenate([slot_grad.astype(F32), jnp.zeros((feats - chans, nslots), F32)], axis=0)
-    sgs[...] = wide.T.astype(BF16).reshape(sgs.shape)
-    spread(sgs, sgr, rev_sem)
     proj_part = jnp.dot(slot_grad, arrived, preferred_element_type=F32)
     for t in range(8):
         ptiles[t // per, t % per] = proj_part[8 * t : 8 * t + 8]
@@ -415,6 +412,10 @@
         @pl.when(me != d)
         def _(m=m, d=d):
             remote(ptiles.at[m], prs.at[me], prs_sem.at[0], prs_sem.at[1], d).start()
+
+    wide = jnp.concatenate([slot_grad.astype(F32), jnp.zeros((feats - chans, nslots), F32)], axis=0)
+    sgs[...] = wide.T.astype(BF16).reshape(sgs.shape)
+    spread(sgs, sgr, rev_sem)
 
     waits(rs, rs, rs_sem, half - 1).wait_recv()
     rs[pl.ds(chip, 1)] = tiles[core, pl.ds(chip, 1)]

time: 69.4 us -> 68.1 us (0.981)
  Pallas kernels: 68.6 us -> 67.3 us
    pallas_call x1, Pallas kernels: 66.1 us -> 64.8 us  [local(): pl.pallas_call(functools.partial(kernel, ngx, ngy), out_shape=(jax.ShapeD...]
where the time goes in v5:
time: 68.1 us; the launch traced here: 68 us
  Pallas kernels  67.3 us (99%)
    pallas_call x1, Pallas kernels, local(): pl.pallas_call(functools.partial(kernel, ngx, ngy), out_shape=(jax.ShapeD...  64.8 us
    pallas_call x1, Pallas kernels, local(): pl.pallas_call(functools.partial(ending, 1.0 / math.sqrt(cy * nz * n), 1....  2.58 us

profile of v5, /device:TPU:1, one launch (start us, length us, event | category | flops | bytes accessed | tf_op | source)
XLA Modules:
  0.0 68.0 jit_solution(17148595491079878226)
XLA Ops:
  0.6 64.8 %section.1 = (bf16[1024,256]{1,0:T(8,128)(2,1)}, f32[512,128]{1,0:T(8,128)}, f32[120,1,8,128]{3,2,1,0:T(8,128)}, f32[64,128]{1,0:T(8,128)}) custom-call(s32[1,128]{1,0:T(1,128)} %counts_ref.1, s32[1,1024]{1,0:T(1,128)} %cells_ref.1, bf16[512,128]{1,0:T(8,128)(2,1)} %rows_ref.1, bf16[1024,256]{1,0:T(8,128)(2,1)} %bitcast.7, bf16[1024,256]{1,0:T(8,128)(2,1)} %bitcast.8, ...), custom_call_target="tpu_custom_call" | custom-call | tf_op jit(solution)/shard_map/section/pallas_call | solution.py:510
  65.4 2.6 %ending.1 = (bf16[1024,256]{1,0:T(8,128)(2,1)}, f32[512,128]{1,0:T(8,128)}, f32[27,64,64]{2,1,0:T(8,128)}, f32[64,128]{1,0:T(8,128)}) custom-call(f32[512,128]{1,0:T(8,128)} %get-tuple-element.12.rows_ref, f32[120,1,8,128]{3,2,1,0:T(8,128)} %get-tuple-element.13.sums_ref, f32[64,128]{1,0:T(8,128)} %get-tuple-element.14.psum_ref, ...), custom_call_target="tpu_custom_call" | custom-call | tf_op jit(solution)/shard_map/ending/pallas_call | solution.py:583

commit v6 on v5

--- a/solution.py
+++ b/solution.py
@@ -369,15 +369,14 @@
 
     tap_terms(late_slabs, late_threes)
     per_row = acc.shape[1] // 128
-    proj_shares = 8 // per
+    proj_shares, prow, _ = ptiles.shape
     stride = n // proj_shares
-    proj_at = [stride * m + 5 * (m % 4) for m in range(proj_shares)]
-    conv_at = [d for d in range(n) if d not in proj_at]
+    proj_at = [stride * m + m % stride for m in range(proj_shares)]
     for t in range(120):
         r, q = divmod(t, per_row)
-        d = conv_at[t // per]
+        d = t // per
         tiles[d % 2, d // 2, t % per] = acc[8 * r : 8 * r + 8, 128 * q : 128 * q + 128]
-    for d in proj_at:
+    for d in range(120 // per, n):
         tiles[d % 2, d // 2] = jnp.zeros((per, 8, 128), F32)
     pair_copy = remote(
         tiles.at[1 - core], pair_in, pair_sem.at[0], pair_sem.at[1], me + 1 - 2 * core
@@ -403,10 +402,10 @@
 
     slot_grad = slot_grad.astype(BF16)
     proj_part = jnp.dot(slot_grad, arrived, preferred_element_type=F32)
-    for t in range(8):
-        ptiles[t // per, t % per] = proj_part[8 * t : 8 * t + 8]
+    for m in range(proj_shares):
+        ptiles[m] = proj_part[prow * m : prow * m + prow]
     group = me // stride
-    proj_owner = me % stride == 5 * (group % 4)
+    proj_owner = me % stride == group % stride
     for m, d in enumerate(proj_at):
 
         @pl.when(me != d)
@@ -448,7 +447,7 @@
         ag.at[core], ag.at[1 - core], share_sem.at[0], share_sem.at[1], me + 1 - 2 * core
     ).wait()
     for t in range(120):
-        d = conv_at[t // per]
+        d = t // per
         sums_ref[t // per, t % per] = ag[d % 2, d // 2, t % per]
 
     @pl.when(proj_owner)
@@ -463,8 +462,8 @@
         waits(ptiles, ptiles, prs_sem, proj_shares).wait_send()
         waits(ptiles, ptiles, pag_sem, proj_shares).wait_recv()
 
-    for t in range(8):
-        psum_ref[8 * t : 8 * t + 8] = pag[t // per, t % per]
+    for m in range(proj_shares):
+        psum_ref[prow * m : prow * m + prow] = pag[m]
 
     waits(send, arr, a2a_sem, n - 1).wait_send()
     waits(sgs, sgr, rev_sem, n - 1).wait_send()
@@ -503,6 +502,7 @@
     full = chans * cy
     cap = nslots // n
     per = 128 // n
+    pcount = min(n, 32)
     weight_t = proj_weight.T
     dma = pltpu.SemaphoreType.DMA
     vmem = pl.BlockSpec(memory_space=pltpu.VMEM)
@@ -545,9 +545,9 @@
             pltpu.VMEM((n // 2, per, 8, 128), F32),
             pltpu.VMEM((n // 2, per, 8, 128), F32),
             pltpu.VMEM((2, n // 2, per, 8, 128), F32),
-            pltpu.VMEM((8 // per, per, 8, 128), F32),
-            pltpu.VMEM((n, per, 8, 128), F32),
-            pltpu.VMEM((8 // per, per, 8, 128), F32),
+            pltpu.VMEM((pcount, chans // pcount, feats), F32),
+            pltpu.VMEM((n, chans // pcount, feats), F32),
+            pltpu.VMEM((pcount, chans // pcount, feats), F32),
             pltpu.VMEM((n, cap, feats), BF16),
             pltpu.VMEM((n, cap, feats), BF16),
             dma((2,)),

time: 68.1 us -> 68.5 us (level)
  no operation moved by 1% of the time
where the time goes in v6:
time: 68.5 us; the launch traced here: 68.3 us
  Pallas kernels  67.7 us (99%)
    pallas_call x1, Pallas kernels, local(): pl.pallas_call(functools.partial(kernel, ngx, ngy), out_shape=(jax.ShapeD...  65.1 us
    pallas_call x1, Pallas kernels, local(): pl.pallas_call(functools.partial(ending, 1.0 / math.sqrt(cy * nz * n), 1....  2.58 us

profile of v6, /device:TPU:1, one launch (start us, length us, event | category | flops | bytes accessed | tf_op | source)
XLA Modules:
  0.0 68.3 jit_solution(862046925254823182)
XLA Ops:
  0.6 65.1 %section.1 = (bf16[1024,256]{1,0:T(8,128)(2,1)}, f32[512,128]{1,0:T(8,128)}, f32[120,1,8,128]{3,2,1,0:T(8,128)}, f32[64,128]{1,0:T(8,128)}) custom-call(s32[1,128]{1,0:T(1,128)} %counts_ref.1, s32[1,1024]{1,0:T(1,128)} %cells_ref.1, bf16[512,128]{1,0:T(8,128)(2,1)} %rows_ref.1, bf16[1024,256]{1,0:T(8,128)(2,1)} %bitcast.7, bf16[1024,256]{1,0:T(8,128)(2,1)} %bitcast.8, ...), custom_call_target="tpu_custom_call" | custom-call | tf_op jit(solution)/shard_map/section/pallas_call | solution.py:510
  65.8 2.6 %ending.1 = (bf16[1024,256]{1,0:T(8,128)(2,1)}, f32[512,128]{1,0:T(8,128)}, f32[27,64,64]{2,1,0:T(8,128)}, f32[64,128]{1,0:T(8,128)}) custom-call(f32[512,128]{1,0:T(8,128)} %get-tuple-element.12.rows_ref, f32[120,1,8,128]{3,2,1,0:T(8,128)} %get-tuple-element.13.sums_ref, f32[64,128]{1,0:T(8,128)} %get-tuple-element.14.psum_ref, ...), custom_call_target="tpu_custom_call" | custom-call | tf_op jit(solution)/shard_map/ending/pallas_call | solution.py:583

commit v7 on v5

--- a/solution.py
+++ b/solution.py
@@ -309,7 +309,7 @@
                 grads[x, y] = got.astype(BF16)
 
     def tap_terms(slabs, threes):
-        acc[:, : N_TAPS * chans] += nt_dot(
+        acc[:, : N_TAPS * chans] = nt_dot(
             jnp.concatenate(threes, axis=1), jnp.concatenate(slabs, axis=1)
         )
 
@@ -345,11 +345,8 @@
             threes.append(three.astype(BF16))
         if c < 2:
             g_edges[1 - c].start()
-        if c < 2:
-            tap_terms(slabs, threes)
-        else:
-            late_slabs += slabs
-            late_threes += threes
+        late_slabs += slabs
+        late_threes += threes
         if c == 3:
             for copy in g_edges:
                 copy.wait_recv()
@@ -393,10 +390,6 @@
                 tiles.at[core, peer // 2], rs.at[chip], rs_sem.at[0], rs_sem.at[1], peer
             ).start()
 
-    out_ref[...] = jnp.dot(
-        perm_back[...], outs[...].reshape(full, nz), preferred_element_type=F32
-    ).astype(BF16)
-
     for copy in near_copies:
         copy.wait()
     slot_grad = slot_grad + near_in[0].astype(F32) + near_in[1].astype(F32)
@@ -432,6 +425,10 @@
         pag[pl.ds(group, 1)] = jnp.sum(prs[...], axis=0, keepdims=True)
         for peer, _ in peers:
             remote(pag.at[group], pag.at[group], pag_sem.at[0], pag_sem.at[1], peer).start()
+
+    out_ref[...] = jnp.dot(
+        perm_back[...], outs[...].reshape(full, nz), preferred_element_type=F32
+    ).astype(BF16)
 
     waits(rs, rs, ag_sem, half - 1).wait_recv()
     share_copy = remote(

time: 68.1 us -> 68.1 us (level)
  no operation moved by 1% of the time
where the time goes in v7:
time: 68.1 us; the launch traced here: 68 us
  Pallas kernels  67.3 us (99%)
    pallas_call x1, Pallas kernels, local(): pl.pallas_call(functools.partial(kernel, ngx, ngy), out_shape=(jax.ShapeD...  64.8 us
    pallas_call x1, Pallas kernels, local(): pl.pallas_call(functools.partial(ending, 1.0 / math.sqrt(cy * nz * n), 1....  2.58 us

profile of v7, /device:TPU:1, one launch (start us, length us, event | category | flops | bytes accessed | tf_op | source)
XLA Modules:
  0.0 68.0 jit_solution(18284996299613865473)
XLA Ops:
  0.6 64.8 %section.1 = (bf16[1024,256]{1,0:T(8,128)(2,1)}, f32[512,128]{1,0:T(8,128)}, f32[120,1,8,128]{3,2,1,0:T(8,128)}, f32[64,128]{1,0:T(8,128)}) custom-call(s32[1,128]{1,0:T(1,128)} %counts_ref.1, s32[1,1024]{1,0:T(1,128)} %cells_ref.1, bf16[512,128]{1,0:T(8,128)(2,1)} %rows_ref.1, bf16[1024,256]{1,0:T(8,128)(2,1)} %bitcast.7, bf16[1024,256]{1,0:T(8,128)(2,1)} %bitcast.8, ...), custom_call_target="tpu_custom_call" | custom-call | tf_op jit(solution)/shard_map/section/pallas_call | solution.py:507
  65.4 2.6 %ending.1 = (bf16[1024,256]{1,0:T(8,128)(2,1)}, f32[512,128]{1,0:T(8,128)}, f32[27,64,64]{2,1,0:T(8,128)}, f32[64,128]{1,0:T(8,128)}) custom-call(f32[512,128]{1,0:T(8,128)} %get-tuple-element.12.rows_ref, f32[120,1,8,128]{3,2,1,0:T(8,128)} %get-tuple-element.13.sums_ref, f32[64,128]{1,0:T(8,128)} %get-tuple-element.14.psum_ref, ...), custom_call_target="tpu_custom_call" | custom-call | tf_op jit(solution)/shard_map/ending/pallas_call | solution.py:580

commit v8 on v5

--- a/solution.py
+++ b/solution.py
@@ -393,10 +393,6 @@
                 tiles.at[core, peer // 2], rs.at[chip], rs_sem.at[0], rs_sem.at[1], peer
             ).start()
 
-    out_ref[...] = jnp.dot(
-        perm_back[...], outs[...].reshape(full, nz), preferred_element_type=F32
-    ).astype(BF16)
-
     for copy in near_copies:
         copy.wait()
     slot_grad = slot_grad + near_in[0].astype(F32) + near_in[1].astype(F32)
@@ -432,6 +428,10 @@
         pag[pl.ds(group, 1)] = jnp.sum(prs[...], axis=0, keepdims=True)
         for peer, _ in peers:
             remote(pag.at[group], pag.at[group], pag_sem.at[0], pag_sem.at[1], peer).start()
+
+    out_ref[...] = jnp.dot(
+        perm_back[...], outs[...].reshape(full, nz), preferred_element_type=F32
+    ).astype(BF16)
 
     waits(rs, rs, ag_sem, half - 1).wait_recv()
     share_copy = remote(

time: 68.1 us -> 68.2 us (level)
  no operation moved by 1% of the time
where the time goes in v8:
time: 68.2 us; the launch traced here: 68.1 us
  Pallas kernels  67.4 us (99%)
    pallas_call x1, Pallas kernels, local(): pl.pallas_call(functools.partial(kernel, ngx, ngy), out_shape=(jax.ShapeD...  64.8 us
    pallas_call x1, Pallas kernels, local(): pl.pallas_call(functools.partial(ending, 1.0 / math.sqrt(cy * nz * n), 1....  2.58 us

profile of v8, /device:TPU:1, one launch (start us, length us, event | category | flops | bytes accessed | tf_op | source)
XLA Modules:
  0.0 68.1 jit_solution(10799755553379115105)
XLA Ops:
  0.6 64.8 %section.1 = (bf16[1024,256]{1,0:T(8,128)(2,1)}, f32[512,128]{1,0:T(8,128)}, f32[120,1,8,128]{3,2,1,0:T(8,128)}, f32[64,128]{1,0:T(8,128)}) custom-call(s32[1,128]{1,0:T(1,128)} %counts_ref.1, s32[1,1024]{1,0:T(1,128)} %cells_ref.1, bf16[512,128]{1,0:T(8,128)(2,1)} %rows_ref.1, bf16[1024,256]{1,0:T(8,128)(2,1)} %bitcast.7, bf16[1024,256]{1,0:T(8,128)(2,1)} %bitcast.8, ...), custom_call_target="tpu_custom_call" | custom-call | tf_op jit(solution)/shard_map/section/pallas_call | solution.py:510
  65.5 2.6 %ending.1 = (bf16[1024,256]{1,0:T(8,128)(2,1)}, f32[512,128]{1,0:T(8,128)}, f32[27,64,64]{2,1,0:T(8,128)}, f32[64,128]{1,0:T(8,128)}) custom-call(f32[512,128]{1,0:T(8,128)} %get-tuple-element.12.rows_ref, f32[120,1,8,128]{3,2,1,0:T(8,128)} %get-tuple-element.13.sums_ref, f32[64,128]{1,0:T(8,128)} %get-tuple-element.14.psum_ref, ...), custom_call_target="tpu_custom_call" | custom-call | tf_op jit(solution)/shard_map/ending/pallas_call | solution.py:583
